TPU v7x, 32 devices: a whole 2x2x4 slice. The times are simulated.
32 devices in a mesh: dp: 8 (over z, x), ctx: 4 (over y, core).
Axes of the slice: x: 2, y: 2, z: 4, core: 2. Of those that a mesh axis runs over, the one named last changes fastest.
Arguments:
- block_input: bfloat16 [8, 512, 1088], P('dp', 'ctx'), may hold values from -6 to 6
- norm_one_gain: bfloat16 [1088], P('dp'), may hold values from 0.099609375 to 1.8984375
- norm_one_bias: bfloat16 [1088], P('dp'), may hold values from -1.796875 to 1.796875
- w_qkv: bfloat16 [1088, 3264], P('ctx', 'dp'), may hold values from -3 to 3
- bias_qv: bfloat16 [2176], P('dp'), may hold values from -1.1953125 to 1.1953125
- w_out: bfloat16 [1088, 1088], P('ctx', 'dp'), may hold values from -1.5 to 1.5
- bias_out: bfloat16 [1088], P('dp'), may hold values from -1.796875 to 1.796875
- norm_two_gain: bfloat16 [1088], P('dp'), may hold values from 0.099609375 to 1.8984375
- norm_two_bias: bfloat16 [1088], P('dp'), may hold values from -1.796875 to 1.796875
- w_up: bfloat16 [1088, 4352], P('ctx', 'dp'), may hold values from -0.1875 to 0.1875
- bias_up: bfloat16 [4352], P('dp'), may hold values from -1.796875 to 1.796875
- w_down: bfloat16 [4352, 1088], P('ctx', 'dp'), may hold values from -0.09375 to 0.09375
- bias_down: bfloat16 [1088], P('dp'), may hold values from -1.796875 to 1.796875
- cotangent: bfloat16 [8, 512, 1088], P('dp', 'ctx'), may hold values from -6 to 6
Outputs:
- block_output: bfloat16 [8, 512, 1088], P('dp', 'ctx')
- grad_input: float32 [8, 512, 1088], P('dp', 'ctx')
- grad_norm_one_gain: float32 [1088], P('dp')
- grad_norm_one_bias: float32 [1088], P('dp')
- grad_w_qkv: float32 [1088, 3264], P('ctx', 'dp')
- grad_bias_qv: float32 [2176], P('dp')
- grad_w_out: float32 [1088, 1088], P('ctx', 'dp')
- grad_bias_out: float32 [1088], P('dp')
- grad_norm_two_gain: float32 [1088], P('dp')
- grad_norm_two_bias: float32 [1088], P('dp')
- grad_w_up: float32 [1088, 4352], P('ctx', 'dp')
- grad_bias_up: float32 [4352], P('dp')
- grad_w_down: float32 [4352, 1088], P('ctx', 'dp')
- grad_bias_down: float32 [1088], P('dp')
All inputs are finite; a program needn't handle non-finite values.
Results may differ from a plain program's by a relative error of at most 0.01.
Values may be sent and summed in bfloat16 or wider, within the bound.
A program may use at most 192 MiB of HBM per device.

v0:
```python
import jax
import jax.numpy as jnp
from jax import lax
from jax.sharding import PartitionSpec as P

HEADS = 17
HEAD_DIM = 64


EPS = 1e-05
MASKED = -1e30
INV_ROOT_TWO = 0.7071067811865476
INV_ROOT_TWO_PI = 0.3989422804014327


def norm_forward(rows_in, gain, shift):
    center = jnp.mean(rows_in, axis=-1, keepdims=True)
    offset = rows_in - center
    spread = jnp.mean(offset * offset, axis=-1, keepdims=True)
    inverse = lax.rsqrt(spread + EPS)
    scaled = offset * inverse
    normed = (scaled * gain.astype(jnp.float32) + shift.astype(jnp.float32)).astype(jnp.bfloat16)
    return (scaled, inverse, normed)


def norm_backward(upstream, scaled, inverse, gain):
    weighted = upstream * gain.astype(jnp.float32)
    first = jnp.mean(weighted, axis=-1, keepdims=True)
    second = jnp.mean(weighted * scaled, axis=-1, keepdims=True)
    return inverse * (weighted - first - scaled * second)


def gelu_value(pre):
    return 0.5 * pre * (1.0 + lax.erf(pre * INV_ROOT_TWO))


def gelu_slope(pre):
    return (
        0.5 * (1.0 + lax.erf(pre * INV_ROOT_TWO))
        + pre * jnp.exp(-0.5 * pre * pre) * INV_ROOT_TWO_PI
    )


def inner_rows(left, right):
    return lax.dot_general(
        left, right, (((0,), (0,)), ((), ())), preferred_element_type=jnp.float32
    )


def outer_cols(left, right):
    return lax.dot_general(
        left, right, (((1,), (1,)), ((), ())), preferred_element_type=jnp.float32
    )


def head_view(block):
    return block.reshape(block.shape[0], block.shape[1], HEADS, HEAD_DIM)


def masked_scores(query_heads, key_heads, allowed, factor):
    scores = (
        jnp.einsum("sqhd,skhd->shqk", query_heads, key_heads, preferred_element_type=jnp.float32)
        * factor
    )
    return jnp.where(allowed, scores, MASKED)


def on_device(
    block_input,
    norm_one_gain,
    norm_one_bias,
    w_qkv,
    bias_qv,
    w_out,
    bias_out,
    norm_two_gain,
    norm_two_bias,
    w_up,
    bias_up,
    w_down,
    bias_down,
    cotangent,
):
    seq_count, block_len, width = block_input.shape
    row_count = seq_count * block_len
    ctx_count = lax.axis_size("ctx")
    seq_len = block_len * ctx_count
    grad_scale = float(row_count * lax.axis_size("dp") * ctx_count) ** (-0.5)
    factor = float(HEAD_DIM) ** (-0.5)
    row_pieces = (
        lax.all_gather(w_qkv, "ctx", axis=0, tiled=True),
        lax.all_gather(w_out, "ctx", axis=0, tiled=True),
        lax.all_gather(w_up, "ctx", axis=0, tiled=True),
        lax.all_gather(w_down, "ctx", axis=0, tiled=True),
    )
    gathered = (
        lax.all_gather(row_pieces[0], "dp", axis=1, tiled=True),
        lax.all_gather(row_pieces[1], "dp", axis=1, tiled=True),
        lax.all_gather(row_pieces[2], "dp", axis=1, tiled=True),
        lax.all_gather(row_pieces[3], "dp", axis=1, tiled=True),
        lax.all_gather(norm_one_gain, "dp", axis=0, tiled=True),
        lax.all_gather(norm_one_bias, "dp", axis=0, tiled=True),
        lax.all_gather(bias_qv, "dp", axis=0, tiled=True),
        lax.all_gather(bias_out, "dp", axis=0, tiled=True),
        lax.all_gather(norm_two_gain, "dp", axis=0, tiled=True),
        lax.all_gather(norm_two_bias, "dp", axis=0, tiled=True),
        lax.all_gather(bias_up, "dp", axis=0, tiled=True),
        lax.all_gather(bias_down, "dp", axis=0, tiled=True),
    )
    matrices = gathered[:4]
    vectors = gathered[4:]
    full_qkv, full_out, full_up, full_down = matrices
    (
        gain_one,
        shift_one,
        full_bias_qv,
        full_bias_out,
        gain_two,
        shift_two,
        full_bias_up,
        full_bias_down,
    ) = vectors
    inputs = block_input.reshape(row_count, width).astype(jnp.float32)
    scaled_one, inverse_one, normed_one = norm_forward(inputs, gain_one, shift_one)
    bias_float = full_bias_qv.astype(jnp.float32)
    qkv_bias = jnp.concatenate(
        [bias_float[:width], jnp.zeros((width,), jnp.float32), bias_float[width:]]
    )
    projected = (
        jnp.dot(normed_one, full_qkv, preferred_element_type=jnp.float32) + qkv_bias
    ).astype(jnp.bfloat16)
    queries = projected[:, :width].reshape(seq_count, block_len, width)
    keys_here = projected[:, width : 2 * width].reshape(seq_count, block_len, width)
    values_here = projected[:, 2 * width :].reshape(seq_count, block_len, width)
    keys_all, values_all = (
        lax.all_gather(keys_here, "ctx", axis=1, tiled=True),
        lax.all_gather(values_here, "ctx", axis=1, tiled=True),
    )
    query_heads = head_view(queries)
    key_heads = head_view(keys_all)
    value_heads = head_view(values_all)
    query_index = lax.axis_index("ctx") * block_len + jnp.arange(block_len, dtype=jnp.int32)
    key_index = jnp.arange(seq_len, dtype=jnp.int32)
    allowed = key_index[None, :] <= query_index[:, None]
    scores = masked_scores(query_heads, key_heads, allowed, factor)
    peak = jnp.max(scores, axis=-1, keepdims=True)
    log_total = peak + jnp.log(jnp.sum(jnp.exp(scores - peak), axis=-1, keepdims=True))
    soft_weights = jnp.exp(scores - log_total).astype(jnp.bfloat16)
    mixed = jnp.einsum(
        "shqk,skhd->sqhd", soft_weights, value_heads, preferred_element_type=jnp.float32
    ).astype(jnp.bfloat16)
    mixed_rows = mixed.reshape(row_count, width)
    residual = inputs + (
        jnp.dot(mixed_rows, full_out, preferred_element_type=jnp.float32)
        + full_bias_out.astype(jnp.float32)
    )
    scaled_two, inverse_two, normed_two = norm_forward(residual, gain_two, shift_two)
    hidden_pre = jnp.dot(
        normed_two, full_up, preferred_element_type=jnp.float32
    ) + full_bias_up.astype(jnp.float32)
    hidden = gelu_value(hidden_pre).astype(jnp.bfloat16)
    result = residual + (
        jnp.dot(hidden, full_down, preferred_element_type=jnp.float32)
        + full_bias_down.astype(jnp.float32)
    )
    block_output = result.astype(jnp.bfloat16).reshape(seq_count, block_len, width)
    upstream = cotangent.reshape(row_count, width)
    up_float = upstream.astype(jnp.float32)
    grad_bias_down = jnp.sum(up_float, axis=0)
    grad_hidden = outer_cols(upstream, full_down) * gelu_slope(hidden_pre)
    grad_hidden_low = grad_hidden.astype(jnp.bfloat16)
    grad_bias_up = jnp.sum(grad_hidden, axis=0)
    grad_normed_two = outer_cols(grad_hidden_low, full_up)
    grad_gain_two = jnp.sum(grad_normed_two * scaled_two, axis=0)
    grad_shift_two = jnp.sum(grad_normed_two, axis=0)
    grad_residual = up_float + norm_backward(grad_normed_two, scaled_two, inverse_two, gain_two)
    grad_residual_low = grad_residual.astype(jnp.bfloat16)
    grad_bias_out = jnp.sum(grad_residual, axis=0)
    grad_mixed = (
        outer_cols(grad_residual_low, full_out)
        .astype(jnp.bfloat16)
        .reshape(seq_count, block_len, HEADS, HEAD_DIM)
    )
    scores_again = masked_scores(query_heads, key_heads, allowed, factor)
    probs = jnp.exp(scores_again - log_total)
    soft_again = probs.astype(jnp.bfloat16)
    grad_probs = jnp.einsum(
        "sqhd,skhd->shqk", grad_mixed, value_heads, preferred_element_type=jnp.float32
    )
    delta = jnp.einsum("sqhd,sqhd->shq", grad_mixed, mixed, preferred_element_type=jnp.float32)[
        ..., None
    ]
    grad_scores = (probs * (grad_probs - delta) * factor).astype(jnp.bfloat16)
    grad_queries = jnp.einsum(
        "shqk,skhd->sqhd", grad_scores, key_heads, preferred_element_type=jnp.float32
    ).reshape(row_count, width)
    key_part = jnp.einsum(
        "shqk,sqhd->skhd", grad_scores, query_heads, preferred_element_type=jnp.float32
    ).reshape(seq_count, seq_len, width)
    value_part = jnp.einsum(
        "shqk,sqhd->skhd", soft_again, grad_mixed, preferred_element_type=jnp.float32
    ).reshape(seq_count, seq_len, width)
    grad_keys, grad_values = (
        lax.psum_scatter(key_part, "ctx", scatter_dimension=1, tiled=True),
        lax.psum_scatter(value_part, "ctx", scatter_dimension=1, tiled=True),
    )
    grad_keys = grad_keys.reshape(row_count, width)
    grad_values = grad_values.reshape(row_count, width)
    grad_bias_qv = jnp.concatenate([jnp.sum(grad_queries, axis=0), jnp.sum(grad_values, axis=0)])
    grad_projected = jnp.concatenate([grad_queries, grad_keys, grad_values], axis=1).astype(
        jnp.bfloat16
    )
    grad_normed_one = outer_cols(grad_projected, full_qkv)
    grad_gain_one = jnp.sum(grad_normed_one * scaled_one, axis=0)
    grad_shift_one = jnp.sum(grad_normed_one, axis=0)
    grad_input = grad_residual + norm_backward(grad_normed_one, scaled_one, inverse_one, gain_one)
    grad_input = grad_input.reshape(seq_count, block_len, width)
    left_slices = (
        lax.all_to_all(normed_one, "ctx", split_axis=1, concat_axis=0, tiled=True),
        lax.all_to_all(mixed_rows, "ctx", split_axis=1, concat_axis=0, tiled=True),
        lax.all_to_all(normed_two, "ctx", split_axis=1, concat_axis=0, tiled=True),
        lax.all_to_all(hidden, "ctx", split_axis=1, concat_axis=0, tiled=True),
    )
    right_whole = (
        lax.all_gather(grad_projected, "ctx", axis=0, tiled=True),
        lax.all_gather(grad_residual_low, "ctx", axis=0, tiled=True),
        lax.all_gather(grad_hidden_low, "ctx", axis=0, tiled=True),
        lax.all_gather(upstream, "ctx", axis=0, tiled=True),
    )
    part_qkv = inner_rows(left_slices[0], right_whole[0])
    part_out = inner_rows(left_slices[1], right_whole[1])
    part_up = inner_rows(left_slices[2], right_whole[2])
    part_down = inner_rows(left_slices[3], right_whole[3])
    received = (
        lax.all_to_all(part_qkv[None], "dp", split_axis=2, concat_axis=0, tiled=True),
        lax.all_to_all(part_out[None], "dp", split_axis=2, concat_axis=0, tiled=True),
        lax.all_to_all(part_up[None], "dp", split_axis=2, concat_axis=0, tiled=True),
        lax.all_to_all(part_down[None], "dp", split_axis=2, concat_axis=0, tiled=True),
    )
    matrix_parts = tuple((jnp.sum(member, axis=0) for member in received))
    vector_parts = (
        lax.psum_scatter(grad_gain_one, "dp", scatter_dimension=0, tiled=True),
        lax.psum_scatter(grad_shift_one, "dp", scatter_dimension=0, tiled=True),
        lax.psum_scatter(grad_bias_qv, "dp", scatter_dimension=0, tiled=True),
        lax.psum_scatter(grad_bias_out, "dp", scatter_dimension=0, tiled=True),
        lax.psum_scatter(grad_gain_two, "dp", scatter_dimension=0, tiled=True),
        lax.psum_scatter(grad_shift_two, "dp", scatter_dimension=0, tiled=True),
        lax.psum_scatter(grad_bias_up, "dp", scatter_dimension=0, tiled=True),
        lax.psum_scatter(grad_bias_down, "dp", scatter_dimension=0, tiled=True),
    )
    vector_totals = lax.psum(
        (
            vector_parts[0],
            vector_parts[1],
            vector_parts[2],
            vector_parts[3],
            vector_parts[4],
            vector_parts[5],
            vector_parts[6],
            vector_parts[7],
        ),
        "ctx",
    )
    return (
        block_output,
        grad_input,
        vector_totals[0] * grad_scale,
        vector_totals[1] * grad_scale,
        matrix_parts[0] * grad_scale,
        vector_totals[2] * grad_scale,
        matrix_parts[1] * grad_scale,
        vector_totals[3] * grad_scale,
        vector_totals[4] * grad_scale,
        vector_totals[5] * grad_scale,
        matrix_parts[2] * grad_scale,
        vector_totals[6] * grad_scale,
        matrix_parts[3] * grad_scale,
        vector_totals[7] * grad_scale,
    )


def solution(mesh):
    in_specs = (
        P("dp", "ctx", None),
        P("dp"),
        P("dp"),
        P("ctx", "dp"),
        P("dp"),
        P("ctx", "dp"),
        P("dp"),
        P("dp"),
        P("dp"),
        P("ctx", "dp"),
        P("dp"),
        P("ctx", "dp"),
        P("dp"),
        P("dp", "ctx", None),
    )
    out_specs = (
        P("dp", "ctx", None),
        P("dp", "ctx", None),
        P("dp"),
        P("dp"),
        P("ctx", "dp"),
        P("dp"),
        P("ctx", "dp"),
        P("dp"),
        P("dp"),
        P("dp"),
        P("ctx", "dp"),
        P("dp"),
        P("ctx", "dp"),
        P("dp"),
    )
    return jax.shard_map(
        on_device, mesh=mesh, in_specs=in_specs, out_specs=out_specs, check_vma=False
    )
```

profile of v0, /device:TPU:19, one launch (start us, length us, event | category | flops | bytes accessed | tf_op | source)
XLA Modules:
  0.0 1156.4 jit_solution(14338467642909756432)
XLA Ops:
  7.3 11.3 all_gather.68
  26.3 27.5 %all-reduce.18 = (bf16[2176]{0:T(1024)(128)(2,1)S(1)}, bf16[1088]{0:T(1024)(128)(2,1)S(1)}, bf16[1088]{0:T(1024)(128)(2,1)S(1)}, bf16[1088]{0:T(1024)(128)(2,1)S...) all-reduce(bf16[2176]{0:T(1024)(128)(2,1)S(1)} %dynamic-update-slic, ...), channel_id=1, replica_groups=mesh['dp'=8,'ctx'=4] {'dp'}, use_global_device_ids=true, to_apply=%add.2 | all-reduce | flops 13056 | bytes 52224
  54.4 78.4 %all-gather.18.cloned.1.call-done = bf16[1088,3264]{0,1:T(8,128)(2,1)} async-done(((bf16[1088,408]{0,1:T(8,128)(2,1)}), bf16[1088,3264]{0,1:T(8,128)(2,1)}) %all-gather.18.cloned.1.call-update) | async-done | bytes 7102480 | tf_op jit(solution)/shard_map/all_gather | solution.py:97
  139.7 10.0 all-gather.3
  158.2 16.4 %all-gather.40.cloned.1.call-done = bf16[4,1088,136]{1,2,0:T(8,128)(2,1)} async-done(((bf16[1,1088,136]{1,2,0:T(8,128)(2,1)}), bf16[4,1088,136]{1,2,0:T(8,128)(2,1)}) %all-gather.40.cloned.1.call-update) | async-done | bytes 1183760 | tf_op jit(solution)/shard_map/all_gather | solution.py:94
  179.0 14.8 %all-gather.36.cloned.1.call-done = bf16[512,1088]{0,1:T(8,128)(2,1)} async-done(((bf16[128,1088]{0,1:T(8,128)(2,1)}), bf16[512,1088]{0,1:T(8,128)(2,1)}) %all-gather.36.cloned.1.call-update) | async-done | bytes 1114128 | tf_op jit(solution)/shard_map/all_gather | solution.py:136
  198.0 15.0 %all-gather.34.cloned.1.call-done = bf16[512,1088]{0,1:T(8,128)(2,1)} async-done(((bf16[128,1088]{0,1:T(8,128)(2,1)}), bf16[512,1088]{0,1:T(8,128)(2,1)}) %all-gather.34.cloned.1.call-update) | async-done | bytes 1114128 | tf_op jit(solution)/shard_map/all_gather | solution.py:137
  216.9 49.4 %all-gather.20.cloned.1.call-done = bf16[1088,1088]{0,1:T(8,128)(2,1)} async-done(((bf16[1088,136]{0,1:T(8,128)(2,1)}), bf16[1088,1088]{0,1:T(8,128)(2,1)}) %all-gather.20.cloned.1.call-update) | async-done | bytes 2367504 | tf_op jit(solution)/shard_map/all_gather | solution.py:98
  270.1 141.4 %all-gather.24.cloned.1.call-done = bf16[1088,4352]{0,1:T(8,128)(2,1)} async-done(((bf16[1088,544]{0,1:T(8,128)(2,1)}), bf16[1088,4352]{0,1:T(8,128)(2,1)}) %all-gather.24.cloned.1.call-update) | async-done | bytes 9469968 | tf_op jit(solution)/shard_map/all_gather | solution.py:99
  419.7 129.8 %all-gather.26.cloned.1.call-done = bf16[4352,1088]{0,1:T(8,128)(2,1)} async-done(((bf16[4352,136]{0,1:T(8,128)(2,1)}), bf16[4352,1088]{0,1:T(8,128)(2,1)}) %all-gather.26.cloned.1.call-update) | async-done | bytes 9469968 | tf_op jit(solution)/shard_map/all_gather | solution.py:100
  568.0 11.9 %all_to_all.121 = bf16[128,4,272]{0,2,1:T(8,128)(2,1)} all-to-all(bf16[128,4,272]{0,2,1:T(8,128)(2,1)S(1)} %add_convert_fusion), channel_id=1, replica_groups=mesh['dp'=8,'ctx'=4] {'ctx'}, dimensions={1} | all-to-all | bytes 557056 | tf_op jit(solution)/shard_map/all_to_all | solution.py:219
  611.8 12.1 %all-to-all-done.6 = bf16[128,4,1088]{0,2,1:T(8,128)(2,1)S(1)} async-done(((bf16[128,4,1088]{0,2,1:T(8,128)(2,1)}), bf16[128,4,1088]{0,2,1:T(8,128)(2,1)S(1)}, u32[]{:S(2)}, u32[]{:S(2)}) %all-to-all-start.6) | async-done | bytes 1114144 | tf_op jit(solution)/shard_map/all_to_all | solution.py:222
  624.0 10.2 all-to-all-start.3
  640.1 12.8 %copy.90 = f32[1,1088,1088]{1,0,2:T(1,128)} copy(f32[1,1088,1088]{2,1,0:T(8,128)} %convolution_bitcast_fusion) | data formatting | bytes 9469952 | tf_op jit(solution)/shard_map/broadcast_in_dim | solution.py:238
  652.9 16.9 %all-to-all-done.3 = f32[1,272,1088]{1,0,2:T(1,128)} async-done(((f32[1,272,1088]{1,0,2:T(1,128)}), f32[1,272,1088]{1,0,2:T(1,128)}, u32[]{:S(2)}, u32[]{:S(2)}) %all-to-all-start.3) | async-done | bytes 1183776 | tf_op jit(solution)/shard_map/all_to_all | solution.py:236
  699.1 14.3 %copy.86 = f32[1,272,4352]{1,0,2:T(1,128)} copy(f32[1,272,4352]{2,1,0:T(8,128)} %convolution_bitcast_fusion.1) | data formatting | bytes 9469952 | tf_op jit(solution)/shard_map/broadcast_in_dim | solution.py:237
  713.4 71.1 %all-to-all-done.7 = f32[1,1088,1088]{1,0,2:T(1,128)} async-done(((f32[1,1088,1088]{1,0,2:T(1,128)}), f32[1,1088,1088]{1,0,2:T(1,128)}, u32[]{:S(2)}, u32[]{:S(2)}) %all-to-all-start.7) | async-done | bytes 4735008 | tf_op jit(solution)/shard_map/all_to_all | solution.py:238
  797.8 32.8 %all-gather.28.cloned.1.call-done = bf16[512,3264]{0,1:T(8,128)(2,1)} async-done(((bf16[128,3264]{0,1:T(8,128)(2,1)}), bf16[512,3264]{0,1:T(8,128)(2,1)}) %all-gather.28.cloned.1.call-update) | async-done | bytes 3342352 | tf_op jit(solution)/shard_map/all_gather | solution.py:225
  835.5 12.0 %copy.81 = f32[1,272,3264]{1,0,2:T(1,128)} copy(f32[1,272,3264]{2,1,0:T(8,128)} %convolution_bitcast_fusion.2) | data formatting | bytes 7102464 | tf_op jit(solution)/shard_map/broadcast_in_dim | solution.py:235
  847.5 87.4 %all-to-all-done.5 = f32[1,272,4352]{1,0,2:T(1,128)} async-done(((f32[1,272,4352]{1,0,2:T(1,128)}), f32[1,272,4352]{1,0,2:T(1,128)}, u32[]{:S(2)}, u32[]{:S(2)}) %all-to-all-start.5) | async-done | bytes 4735008 | tf_op jit(solution)/shard_map/all_to_all | solution.py:237
  960.2 108.8 %all-reduce.16 = (f32[1088]{0:T(1024)S(1)}, f32[1088]{0:T(1024)S(1)}, f32[2176]{0:T(1024)S(1)}, f32[1088]{0:T(1024)S(1)}, f32[1088]{0:T(1024)S(1)}, /*index=5*/f...) all-reduce(f32[1088]{0:T(1024)S(1)} %get-tuple-element.16, ...), channel_id=7, replica_groups=mesh['dp'=8,'ctx'=4] {'dp'}, use_global_device_ids=true, to_apply=%region_13.14.clone | all-reduce | flops 13056 | bytes 104448
  1069.6 14.9 %all-reduce.17 = (f32[136]{0:T(256)S(1)}, f32[136]{0:T(256)S(1)}, f32[272]{0:T(512)S(1)}, f32[136]{0:T(256)S(1)}, f32[136]{0:T(256)S(1)}, /*index=5*/f32[136]{0:T(256)S(1)}, f32[544]{0:T(1024)S(1)}, f32[136]{0:T(256)S(1)}) all-reduce(f32[136]{0:T(256)S(1)} %dynamic-slice.9, ...), channel_id=1, replica_groups=mesh['dp'=8,'ctx'=4] {'ctx'}, use_global_device_ids=true, to_apply=%region_14.15 | all-reduce | flops 1632 | bytes 13056 | tf_op jit(solution)/shard_map/psum | solution.py:251
  1098.7 14.4 %copy.87 = f32[1,272,4352]{2,1,0:T(8,128)} copy(f32[1,272,4352]{1,0,2:T(1,128)} %all-to-all-done.5) | data formatting | bytes 9469952 | tf_op jit(solution)/shard_map/all_to_all | solution.py:237
  1125.8 12.3 %copy.82 = f32[1,272,3264]{2,1,0:T(8,128)} copy(f32[1,272,3264]{1,0,2:T(1,128)} %all-to-all-done.1) | data formatting | bytes 7102464 | tf_op jit(solution)/shard_map/all_to_all | solution.py:235
  (210 shorter events, 212.0 us)
Async XLA Ops:
  7.2 125.6 %all-gather.18.cloned.1.call-start = ((), (), s32[]{:S(2)}) async-start(), calls=%async_computation.10 | async-start | bytes 8460288 | tf_op jit(solution)/shard_map/all_gather | solution.py:97
  20.2 135.3 %all-gather.22.cloned.1.call-start = ((), (), s32[]{:S(2)}) async-start(), calls=%async_computation.12 | async-start | bytes 1740800 | tf_op jit(solution)/shard_map/all_gather | solution.py:93
  20.9 153.6 %all-gather.40.cloned.1.call-start = ((), (), s32[]{:S(2)}) async-start(), calls=%async_computation.23 | async-start | bytes 1566720 | tf_op jit(solution)/shard_map/all_gather | solution.py:94
  21.7 172.1 %all-gather.36.cloned.1.call-start = ((), (), s32[]{:S(2)}) async-start(), calls=%async_computation.21 | async-start | bytes 1392640 | tf_op jit(solution)/shard_map/all_gather | solution.py:136
  139.1 73.9 %all-gather.34.cloned.1.call-start = ((), (), s32[]{:S(2)}) async-start(), calls=%async_computation.20 | async-start | bytes 1392640 | tf_op jit(solution)/shard_map/all_gather | solution.py:137
  139.7 126.6 %all-gather.20.cloned.1.call-start = ((), (), s32[]{:S(2)}) async-start(), calls=%async_computation.11 | async-start | bytes 2820096 | tf_op jit(solution)/shard_map/all_gather | solution.py:98
  150.9 260.6 %all-gather.24.cloned.1.call-start = ((), (), s32[]{:S(2)}) async-start(), calls=%async_computation.13 | async-start | bytes 11280384 | tf_op jit(solution)/shard_map/all_gather | solution.py:99
  158.1 391.4 %all-gather.26.cloned.1.call-start = ((), (), s32[]{:S(2)}) async-start(), calls=%async_computation.14 | async-start | bytes 10653696 | tf_op jit(solution)/shard_map/all_gather | solution.py:100
  178.3 428.2 %all-gather.30.cloned.1.call-start = ((), (), s32[]{:S(2)}) async-start(), calls=%async_computation.18 | async-start | bytes 1392640 | tf_op jit(solution)/shard_map/all_gather | solution.py:226
  270.1 279.4 %copy-start.8 = (bf16[1,128,1088]{1,2,0:T(8,128)(2,1)S(1)}, bf16[1,128,1088]{1,2,0:T(8,128)(2,1)}, u32[]{:S(2)}) copy-start(bf16[1,128,1088]{1,2,0:T(8,128)(2,1)} %param.27) | copy-start | bytes 835588
  419.7 173.4 %copy-start.2 = (bf16[128,4352]{1,0:T(8,128)(2,1)}, bf16[128,4352]{1,0:T(8,128)(2,1)S(1)}, u32[]{:S(2)}) copy-start(bf16[128,4352]{1,0:T(8,128)(2,1)S(1)} %get-tuple-element.66) | copy-start | bytes 3342340
  566.2 68.7 %all-gather.38.cloned.1.call-start = ((), (), s32[]{:S(2)}) async-start(), calls=%async_computation.22 | async-start | bytes 1392640 | tf_op jit(solution)/shard_map/all_gather | solution.py:228
  566.7 125.0 %all-gather.32.cloned.1.call-start = ((), (), s32[]{:S(2)}) async-start(), calls=%async_computation.19 | async-start | bytes 5570560 | tf_op jit(solution)/shard_map/all_gather | solution.py:227
  589.2 12.5 %all-to-all-start.4 = ((bf16[128,4,272]{0,2,1:T(8,128)(2,1)}), bf16[128,4,272]{0,2,1:T(8,128)(2,1)S(1)}, u32[]{:S(2)}, u32[]{:S(2)}) async-start(bf16[128,4,272]{0,2,1:T(8,128)(2,1)} %bitcast.41), calls=%async_computation.6 | async-start | bytes 557056 | tf_op jit(solution)/shard_map/all_to_all | solution.py:221
  602.4 21.6 %all-to-all-start.6 = ((bf16[128,4,1088]{0,2,1:T(8,128)(2,1)}), bf16[128,4,1088]{0,2,1:T(8,128)(2,1)S(1)}, u32[]{:S(2)}, u32[]{:S(2)}) async-start(bf16[128,4,1088]{0,2,1:T(8,128)(2,1)} %bitcast.153), calls=%async_computation.8 | async-start | bytes 2228224 | tf_op jit(solution)/shard_map/all_to_all | solution.py:222
  624.0 45.8 %all-to-all-start.3 = ((f32[1,272,1088]{1,0,2:T(1,128)}), f32[1,272,1088]{1,0,2:T(1,128)}, u32[]{:S(2)}, u32[]{:S(2)}) async-start(f32[1,272,1088]{1,0,2:T(1,128)} %copy.84), calls=%async_computation.5 | async-start | bytes 3342336 | tf_op jit(solution)/shard_map/all_to_all | solution.py:236
  669.8 114.6 %all-to-all-start.7 = ((f32[1,1088,1088]{1,0,2:T(1,128)}), f32[1,1088,1088]{1,0,2:T(1,128)}, u32[]{:S(2)}, u32[]{:S(2)}) async-start(f32[1,1088,1088]{1,0,2:T(1,128)} %copy.90), calls=%async_computation.9 | async-start | bytes 10027008 | tf_op jit(solution)/shard_map/all_to_all | solution.py:238
  677.1 117.1 %reduce-scatter.5.cloned.1.call-start = ((), (), s32[]{:S(2)}) async-start(), calls=%async_computation.16 | async-start | bytes 2785280 | tf_op jit(solution)/shard_map/reduce_scatter | solution.py:205
  684.2 111.5 %reduce-scatter.3.cloned.1.call-start = ((), (), s32[]{:S(2)}) async-start(), calls=%async_computation.15 | async-start | bytes 2785280 | tf_op jit(solution)/shard_map/reduce_scatter | solution.py:204
  784.4 150.4 %all-to-all-start.5 = ((f32[1,272,4352]{1,0,2:T(1,128)}), f32[1,272,4352]{1,0,2:T(1,128)}, u32[]{:S(2)}, u32[]{:S(2)}) async-start(f32[1,272,4352]{1,0,2:T(1,128)} %copy.86), calls=%async_computation.7 | async-start | bytes 13369344 | tf_op jit(solution)/shard_map/all_to_all | solution.py:237
  791.8 38.8 %all-gather.28.cloned.1.call-start = ((), (), s32[]{:S(2)}) async-start(), calls=%async_computation.17 | async-start | bytes 4177920 | tf_op jit(solution)/shard_map/all_gather | solution.py:225
  847.5 96.8 %copy-start.3 = (bf16[128,4352]{1,0:T(8,128)(2,1)S(1)}, bf16[128,4352]{1,0:T(8,128)(2,1)}, u32[]{:S(2)}) copy-start(bf16[128,4352]{1,0:T(8,128)(2,1)} %copy-done.2) | copy-start | bytes 3342340
  934.9 190.9 %all-to-all-start.1 = ((f32[1,272,3264]{1,0,2:T(1,128)}), f32[1,272,3264]{1,0,2:T(1,128)}, u32[]{:S(2)}, u32[]{:S(2)}) async-start(f32[1,272,3264]{1,0,2:T(1,128)} %copy.81), calls=%async_computation.3 | async-start | bytes 10027008 | tf_op jit(solution)/shard_map/all_to_all | solution.py:235
  953.7 135.4 %copy-start.7 = (f32[128,1088]{0,1:T(8,128)S(1)}, f32[128,1088]{0,1:T(8,128)}, u32[]{:S(2)}) copy-start(f32[128,1088]{0,1:T(8,128)} %copy-done.6) | copy-start | bytes 1671172
  (25 other events, 413.3 us)
Sparse Core Ops, SparseCore 0:
  20.3 112.3 all-gather.17
  134.3 21.1 all-gather.21
  157.1 17.4 all-gather.39
  176.5 17.1 all-gather.35
  195.8 17.1 all-gather.33
  215.6 50.6 all-gather.19
  268.4 142.9 all-gather.23
  413.6 135.8 all-gather.25
  566.3 19.5 all-gather.29
  587.3 19.2 all-gather.37
  608.1 38.7 all-gather.31
  684.4 33.7 reduce-scatter.4
  720.8 31.9 reduce-scatter.2
  798.0 32.5 all-gather.27
where the time goes:
time: 1170 us; the launch traced here: 1160 us
  waiting for transfers between devices  680 us (58%)
  blocking collectives  194 us (17%)
  local copies, waits for them, and re-layouts  110 us (9%)
  matrix products  84.9 us (7%)
  starting transfers between devices  41.4 us (4%)
  other arithmetic  27.4 us (2%)
  between operations  18.7 us (2%)
    all_gather x1, waiting for transfers between devices, on_device(): lax.all_gather(row_pieces[2], 'dp', axis=1, tiled=True)  141 us
    unnamed x2, blocking collectives  136 us
    all_gather x1, waiting for transfers between devices, on_device(): lax.all_gather(row_pieces[3], 'dp', axis=1, tiled=True)  130 us
    all_to_all x1, waiting for transfers between devices, on_device(): lax.all_to_all(part_up[None], 'dp', split_axis=2, concat_axis=0, tiled=True)  87.4 us
    all_gather x1, waiting for transfers between devices, on_device(): lax.all_gather(row_pieces[0], 'dp', axis=1, tiled=True)  78.4 us
    all_to_all x1, waiting for transfers between devices, on_device(): lax.all_to_all(part_down[None], 'dp', split_axis=2, concat_axis=0, tiled=...  71.1 us
    all_gather x1, waiting for transfers between devices, on_device(): lax.all_gather(row_pieces[1], 'dp', axis=1, tiled=True)  49.4 us
    all_gather x1, waiting for transfers between devices, on_device(): lax.all_gather(grad_projected, 'ctx', axis=0, tiled=True)  32.8 us
  transfers between devices with their start and end apart: 20, of which 14 were waited for; matrix products, arithmetic and copies ran while one was open for 15% of the time, Pallas kernels for 0%

commit v1 on v0

v1 whole, which is shorter than its diff:
```python
import functools

import jax
import jax.numpy as jnp
from jax import lax
from jax.experimental import pallas as pl
from jax.experimental.pallas import tpu as pltpu
from jax.sharding import PartitionSpec as P

HEADS = 17
HEAD_DIM = 64


EPS = 1e-05
MASKED = -1e30
INV_ROOT_TWO = 0.7071067811865476
INV_ROOT_TWO_PI = 0.3989422804014327


def norm_forward(rows_in, gain, shift):
    center = jnp.mean(rows_in, axis=-1, keepdims=True)
    offset = rows_in - center
    spread = jnp.mean(offset * offset, axis=-1, keepdims=True)
    inverse = lax.rsqrt(spread + EPS)
    scaled = offset * inverse
    normed = (scaled * gain.astype(jnp.float32) + shift.astype(jnp.float32)).astype(jnp.bfloat16)
    return (scaled, inverse, normed)


def norm_backward(upstream, scaled, inverse, gain):
    weighted = upstream * gain.astype(jnp.float32)
    first = jnp.mean(weighted, axis=-1, keepdims=True)
    second = jnp.mean(weighted * scaled, axis=-1, keepdims=True)
    return inverse * (weighted - first - scaled * second)


def gelu_value(pre):
    return 0.5 * pre * (1.0 + lax.erf(pre * INV_ROOT_TWO))


def gelu_slope(pre):
    return (
        0.5 * (1.0 + lax.erf(pre * INV_ROOT_TWO))
        + pre * jnp.exp(-0.5 * pre * pre) * INV_ROOT_TWO_PI
    )


def inner_rows(left, right):
    return lax.dot_general(
        left, right, (((0,), (0,)), ((), ())), preferred_element_type=jnp.float32
    )


def outer_cols(left, right):
    return lax.dot_general(
        left, right, (((1,), (1,)), ((), ())), preferred_element_type=jnp.float32
    )


def head_view(block):
    return block.reshape(block.shape[0], block.shape[1], HEADS, HEAD_DIM)


def masked_scores(query_heads, key_heads, allowed, factor):
    scores = (
        jnp.einsum("sqhd,skhd->shqk", query_heads, key_heads, preferred_element_type=jnp.float32)
        * factor
    )
    return jnp.where(allowed, scores, MASKED)


def greet_all(count):
    me = lax.axis_index("ctx")
    barrier = pltpu.get_barrier_semaphore()
    for step in range(1, count):
        pl.semaphore_signal(
            barrier,
            inc=1,
            device_id={"ctx": lax.rem(me + step, count)},
            device_id_type=pl.DeviceIdType.MESH,
        )
    pl.semaphore_wait(barrier, count - 1)
    return me


def swap_kernel(count, in_ref, out_ref, send_sem, recv_sem):
    me = greet_all(count)
    copies = []
    for step in range(1, count):
        target = lax.rem(me + step, count)
        copy = pltpu.make_async_remote_copy(
            src_ref=in_ref.at[target],
            dst_ref=out_ref.at[me],
            send_sem=send_sem.at[step],
            recv_sem=recv_sem.at[step],
            device_id={"ctx": target},
            device_id_type=pl.DeviceIdType.MESH,
        )
        copy.start()
        copies.append(copy)
    out_ref[pl.ds(me, 1)] = in_ref[pl.ds(me, 1)]
    for copy in copies:
        copy.wait()


def share_kernel(count, in_ref, out_ref, send_sem, recv_sem):
    me = greet_all(count)
    copies = []
    for step in range(1, count):
        copy = pltpu.make_async_remote_copy(
            src_ref=in_ref,
            dst_ref=out_ref.at[me],
            send_sem=send_sem.at[step],
            recv_sem=recv_sem.at[step],
            device_id={"ctx": lax.rem(me + step, count)},
            device_id_type=pl.DeviceIdType.MESH,
        )
        copy.start()
        copies.append(copy)
    out_ref[pl.ds(me, 1)] = in_ref[...][None]
    for copy in copies:
        copy.wait()


def relay_kernel(count, in_ref, out_ref, send_sem, recv_sem):
    me = greet_all(count)
    partner = me + 1 - 2 * lax.rem(me, 2)
    across = lax.rem(me + 2, 4)

    def send(source, slot, sem, target):
        copy = pltpu.make_async_remote_copy(
            src_ref=source,
            dst_ref=out_ref.at[slot],
            send_sem=send_sem.at[sem],
            recv_sem=recv_sem.at[sem],
            device_id={"ctx": target},
            device_id_type=pl.DeviceIdType.MESH,
        )
        copy.start()
        return copy

    far = send(in_ref, me, 1, across)
    near = send(in_ref, me, 2, partner)
    out_ref[pl.ds(me, 1)] = in_ref[...][None]
    far.wait_recv()
    handed = send(out_ref.at[across], across, 3, partner)
    far.wait_send()
    near.wait()
    handed.wait()


def ctx_call(kernel, block, out_shape, ident):
    count = lax.axis_size("ctx")
    return pl.pallas_call(
        functools.partial(kernel, count),
        out_shape=jax.ShapeDtypeStruct(out_shape, block.dtype),
        in_specs=[pl.BlockSpec(memory_space=pltpu.VMEM)],
        out_specs=pl.BlockSpec(memory_space=pltpu.VMEM),
        scratch_shapes=[
            pltpu.SemaphoreType.DMA((count,)),
            pltpu.SemaphoreType.DMA((count,)),
        ],
        compiler_params=pltpu.CompilerParams(collective_id=ident, has_side_effects=True),
        name=f"ctx_exchange_{ident}",
    )(block)


def ctx_swap(block, ident):
    return ctx_call(swap_kernel, block, block.shape, ident)


def ctx_share(block, ident):
    count = lax.axis_size("ctx")
    kernel = relay_kernel if count == 4 else share_kernel
    return ctx_call(kernel, block, (count,) + block.shape, ident)


def on_device(
    block_input,
    norm_one_gain,
    norm_one_bias,
    w_qkv,
    bias_qv,
    w_out,
    bias_out,
    norm_two_gain,
    norm_two_bias,
    w_up,
    bias_up,
    w_down,
    bias_down,
    cotangent,
):
    low = jnp.bfloat16
    seq_count, block_len, width = block_input.shape
    rows = seq_count * block_len
    ctx = lax.axis_size("ctx")
    dp = lax.axis_size("dp")
    fold = dp // ctx
    me = lax.axis_index("ctx")
    seq_len = block_len * ctx
    tokens = rows * ctx
    grad_scale = float(tokens * dp) ** (-0.5)
    factor = float(HEAD_DIM) ** (-0.5)

    there = []
    for d in range(dp):
        for c in range(ctx):
            there.append((d * ctx + c, (fold * c + d % fold) * ctx + d // fold))
    back = [(b, a) for a, b in there]

    def columns_whole(piece):
        moved = lax.ppermute(piece, ("dp", "ctx"), there)
        whole = lax.all_gather(moved, "dp", axis=0, tiled=False)
        whole = whole.reshape(ctx, fold, piece.shape[0], piece.shape[1])
        return whole.transpose(0, 2, 1, 3).reshape(
            ctx * piece.shape[0], fold * piece.shape[1]
        )

    def columns_owned(part, piece):
        parts = part.reshape(ctx, piece.shape[0], fold, piece.shape[1]).transpose(0, 2, 1, 3)
        parts = parts.reshape(dp, piece.shape[0], piece.shape[1]).astype(low)
        mine = lax.psum_scatter(parts, "dp", scatter_dimension=0, tiled=False)
        return lax.ppermute(mine, ("dp", "ctx"), back).astype(jnp.float32) * grad_scale

    def rows_whole(piece):
        return lax.all_gather(piece.T, "dp", axis=0, tiled=True)

    def rows_owned(part):
        mine = lax.psum_scatter(part.astype(low), "dp", scatter_dimension=0, tiled=True)
        return mine.T.astype(jnp.float32) * grad_scale

    shards = (
        norm_one_gain,
        norm_one_bias,
        bias_qv,
        bias_out,
        norm_two_gain,
        norm_two_bias,
        bias_up,
        bias_down,
    )
    sizes = [v.shape[0] for v in shards]
    vectors = lax.all_gather(jnp.concatenate(shards), "dp", axis=0, tiled=False)
    full = []
    at = 0
    for size in sizes:
        full.append(vectors[:, at : at + size].reshape(dp * size).astype(jnp.float32))
        at += size
    (
        gain_one,
        shift_one,
        full_bias_qv,
        full_bias_out,
        gain_two,
        shift_two,
        full_bias_up,
        full_bias_down,
    ) = full

    qkv_c = columns_whole(w_qkv)
    out_c = rows_whole(w_out)
    up_c = columns_whole(w_up)
    down_c = rows_whole(w_down)

    inputs = block_input.reshape(rows, width).astype(jnp.float32)
    scaled_one, inverse_one, normed_one = norm_forward(inputs, gain_one, shift_one)
    normed_one_all = ctx_share(normed_one, 0).reshape(tokens, width)
    qkv_bias = jnp.concatenate(
        [full_bias_qv[:width], jnp.zeros((width,), jnp.float32), full_bias_qv[width:]]
    )
    span = qkv_c.shape[1]
    bias_c = lax.dynamic_slice_in_dim(qkv_bias, me * span, span)
    projected_c = (
        jnp.dot(normed_one_all, qkv_c, preferred_element_type=jnp.float32) + bias_c
    ).astype(low)
    projected = ctx_share(projected_c, 1)
    projected = (
        projected.reshape(ctx, ctx, seq_count, block_len, span)
        .transpose(2, 1, 3, 0, 4)
        .reshape(seq_count, seq_len, 3 * width)
    )
    queries = lax.dynamic_slice_in_dim(projected[:, :, :width], me * block_len, block_len, axis=1)
    query_heads = head_view(queries)
    key_heads = head_view(projected[:, :, width : 2 * width])
    value_heads = head_view(projected[:, :, 2 * width :])
    query_index = me * block_len + jnp.arange(block_len, dtype=jnp.int32)
    key_index = jnp.arange(seq_len, dtype=jnp.int32)
    allowed = key_index[None, :] <= query_index[:, None]
    scores = masked_scores(query_heads, key_heads, allowed, factor)
    peak = jnp.max(scores, axis=-1, keepdims=True)
    log_total = peak + jnp.log(jnp.sum(jnp.exp(scores - peak), axis=-1, keepdims=True))
    probs = jnp.exp(scores - log_total)
    soft_weights = probs.astype(low)
    mixed = jnp.einsum(
        "shqk,skhd->sqhd", soft_weights, value_heads, preferred_element_type=jnp.float32
    ).astype(low)

    slab = width // ctx

    def to_columns(block):
        wide = block.shape[1] // ctx
        swapped = block.reshape(rows, ctx, wide).transpose(1, 0, 2)
        return swapped

    mixed_c = ctx_swap(to_columns(mixed.reshape(rows, width)), 2).reshape(tokens, slab)
    out_part = outer_cols(mixed_c, out_c).astype(low).reshape(ctx, rows, width)
    out_sum = jnp.sum(ctx_swap(out_part, 3).astype(jnp.float32), axis=0)
    residual = inputs + (out_sum + full_bias_out)
    scaled_two, inverse_two, normed_two = norm_forward(residual, gain_two, shift_two)
    upstream = cotangent.reshape(rows, width)
    up_float = upstream.astype(jnp.float32)
    both = ctx_share(jnp.stack([normed_two, upstream]), 4)
    normed_two_all = both[:, 0].reshape(tokens, width)
    upstream_all = both[:, 1].reshape(tokens, width)
    units = up_c.shape[1]
    hidden_pre = jnp.dot(
        normed_two_all, up_c, preferred_element_type=jnp.float32
    ) + lax.dynamic_slice_in_dim(full_bias_up, me * units, units)
    hidden = gelu_value(hidden_pre).astype(low)
    down_part = outer_cols(hidden, down_c).astype(low).reshape(ctx, rows, width)
    grad_hidden = jnp.dot(
        upstream_all, down_c, preferred_element_type=jnp.float32
    ) * gelu_slope(hidden_pre)
    grad_hidden_low = grad_hidden.astype(low)
    normed_part = outer_cols(grad_hidden_low, up_c).astype(low).reshape(ctx, rows, width)
    sums = jnp.sum(
        ctx_swap(jnp.stack([down_part, normed_part], axis=1), 5).astype(jnp.float32), axis=0
    )
    block_output = (
        (residual + (sums[0] + full_bias_down)).astype(low).reshape(seq_count, block_len, width)
    )
    grad_normed_two = sums[1]
    grad_residual = up_float + norm_backward(grad_normed_two, scaled_two, inverse_two, gain_two)
    grad_residual_low = grad_residual.astype(low)
    grad_residual_all = ctx_share(grad_residual_low, 6).reshape(tokens, width)
    grad_mixed_c = jnp.dot(
        grad_residual_all, out_c, preferred_element_type=jnp.float32
    ).astype(low)
    grad_mixed = ctx_swap(grad_mixed_c.reshape(ctx, rows, slab), 7)
    grad_mixed = grad_mixed.transpose(1, 0, 2).reshape(seq_count, block_len, HEADS, HEAD_DIM)
    grad_probs = jnp.einsum(
        "sqhd,skhd->shqk", grad_mixed, value_heads, preferred_element_type=jnp.float32
    )
    delta = jnp.einsum("sqhd,sqhd->shq", grad_mixed, mixed, preferred_element_type=jnp.float32)[
        ..., None
    ]
    grad_scores = (probs * (grad_probs - delta) * factor).astype(low)
    grad_queries = jnp.einsum(
        "shqk,skhd->sqhd", grad_scores, key_heads, preferred_element_type=jnp.float32
    ).reshape(rows, width)
    key_part = jnp.einsum(
        "shqk,sqhd->skhd", grad_scores, query_heads, preferred_element_type=jnp.float32
    )
    value_part = jnp.einsum(
        "shqk,sqhd->skhd", soft_weights, grad_mixed, preferred_element_type=jnp.float32
    )

    def to_blocks(part):
        part = part.astype(low).reshape(seq_count, ctx, block_len, width)
        return part.transpose(1, 0, 2, 3).reshape(ctx, rows, width)

    pairs = jnp.stack([to_blocks(key_part), to_blocks(value_part)], axis=1)
    kv_sums = jnp.sum(ctx_swap(pairs, 8).astype(jnp.float32), axis=0)
    grad_keys, grad_values = kv_sums[0], kv_sums[1]
    grad_projected = jnp.concatenate([grad_queries, grad_keys, grad_values], axis=1).astype(low)
    grad_projected_c = ctx_swap(to_columns(grad_projected), 9).reshape(tokens, span)
    one_part = outer_cols(grad_projected_c, qkv_c).astype(low).reshape(ctx, rows, width)
    grad_normed_one = jnp.sum(ctx_swap(one_part, 10).astype(jnp.float32), axis=0)
    grad_input = grad_residual + norm_backward(grad_normed_one, scaled_one, inverse_one, gain_one)
    grad_input = grad_input.reshape(seq_count, block_len, width)

    grad_down = rows_owned(inner_rows(upstream_all, hidden))
    grad_up = columns_owned(inner_rows(normed_two_all, grad_hidden_low), w_up)
    grad_out = rows_owned(inner_rows(grad_residual_all, mixed_c))
    grad_qkv = columns_owned(inner_rows(normed_one_all, grad_projected_c), w_qkv)

    bias_up_c = jnp.sum(grad_hidden, axis=0)
    grad_bias_up = lax.dynamic_update_slice_in_dim(
        jnp.zeros((ctx * units,), jnp.float32), bias_up_c, me * units, axis=0
    )
    sums_here = (
        jnp.sum(grad_normed_one * scaled_one, axis=0),
        jnp.sum(grad_normed_one, axis=0),
        jnp.concatenate([jnp.sum(grad_queries, axis=0), jnp.sum(grad_values, axis=0)]),
        jnp.sum(grad_residual, axis=0),
        jnp.sum(grad_normed_two * scaled_two, axis=0),
        jnp.sum(grad_normed_two, axis=0),
        grad_bias_up,
        jnp.sum(up_float, axis=0),
    )
    table = jnp.concatenate([v.reshape(dp, -1) for v in sums_here], axis=1)
    table = jnp.sum(ctx_share(table, 11), axis=0)
    totals = lax.psum_scatter(table, "dp", scatter_dimension=0, tiled=False) * grad_scale
    owned = []
    at = 0
    for size in sizes:
        owned.append(totals[at : at + size])
        at += size
    return (
        block_output,
        grad_input,
        owned[0],
        owned[1],
        grad_qkv,
        owned[2],
        grad_out,
        owned[3],
        owned[4],
        owned[5],
        grad_up,
        owned[6],
        grad_down,
        owned[7],
    )


def solution(mesh):
    in_specs = (
        P("dp", "ctx", None),
        P("dp"),
        P("dp"),
        P("ctx", "dp"),
        P("dp"),
        P("ctx", "dp"),
        P("dp"),
        P("dp"),
        P("dp"),
        P("ctx", "dp"),
        P("dp"),
        P("ctx", "dp"),
        P("dp"),
        P("dp", "ctx", None),
    )
    out_specs = (
        P("dp", "ctx", None),
        P("dp", "ctx", None),
        P("dp"),
        P("dp"),
        P("ctx", "dp"),
        P("dp"),
        P("ctx", "dp"),
        P("dp"),
        P("dp"),
        P("dp"),
        P("ctx", "dp"),
        P("dp"),
        P("ctx", "dp"),
        P("dp"),
    )
    return jax.shard_map(
        on_device, mesh=mesh, in_specs=in_specs, out_specs=out_specs, check_vma=False
    )
```

time: 1170 us -> 754 us (0.64)
  the two profiles are of different devices: /device:TPU:19 before, /device:TPU:0 now
where the time goes in v1:
time: 754 us; the launch traced here: 743 us
  Pallas kernels  210 us (28%)
  waiting for transfers between devices  193 us (26%)
  blocking collectives  144 us (19%)
  local copies, waits for them, and re-layouts  88.1 us (12%)
  matrix products  54.3 us (7%)
  other arithmetic  30.4 us (4%)
  between operations  15.9 us (2%)
    pallas_call x12, Pallas kernels, ctx_call(): pl.pallas_call(functools.partial(kernel, count), out_shape=jax.ShapeDtype...  210 us
    unnamed x9, waiting for transfers between devices  120 us
    unnamed x2, blocking collectives  109 us
    reduce_scatter x2, waiting for transfers between devices, columns_owned(): mine = lax.psum_scatter(parts, 'dp', scatter_dimension=0, tiled=False)  73.6 us
    all_gather x1, blocking collectives, rows_whole(): return lax.all_gather(piece.T, 'dp', axis=0, tiled=True)  34.7 us
    dot_general x4, matrix products, inner_rows(): lax.dot_general(left, right, (((0,), (0,)), ((), ())), preferred_element_...  15.2 us
  transfers between devices with their start and end apart: 11, of which 3 were waited for; matrix products, arithmetic and copies ran while one was open for 14% of the time, Pallas kernels for 15%

profile of v1, /device:TPU:0, one launch (start us, length us, event | category | flops | bytes accessed | tf_op | source)
XLA Modules:
  0.0 742.9 jit_solution(12994352880602088348)
XLA Ops:
  14.9 5.5 concatenate.21
  20.7 76.0 %all-reduce = bf16[13056]{0:T(1024)(128)(2,1)S(1)} all-reduce(bf16[13056]{0:T(1024)(128)(2,1)S(1)} %dynamic-update-slice), channel_id=2, replica_groups=mesh['dp'=8,'ctx'=4] {'dp'}, use_global_device_ids=true, to_apply=%add | all-reduce | flops 13056 | bytes 52224
  100.3 34.7 %all_gather.28 = bf16[1088,272]{1,0:T(8,128)(2,1)S(1)} all-gather(bf16[136,272]{1,0:T(8,128)(2,1)S(1)} %bitcast.265), channel_id=1, replica_groups=mesh['dp'=8,'ctx'=4] {'dp'}, dimensions={0}, use_global_device_ids=true | all-gather | bytes 665856 | tf_op jit(solution)/shard_map/all_gather | solution.py:227
  135.9 14.8 %ctx_exchange_0.1 = bf16[4,128,1088]{2,1,0:T(8,128)(2,1)} custom-call(bf16[128,1088]{1,0:T(8,128)(2,1)} %fusion.28.in_ref), custom_call_target="tpu_custom_call" | custom-call | tf_op jit(solution)/shard_map/ctx_exchange_0/pallas_call | solution.py:154
  164.3 27.8 %ctx_exchange_1.1 = bf16[4,512,816]{2,1,0:T(8,128)(2,1)} custom-call(bf16[512,816]{1,0:T(8,128)(2,1)} %add_convert_fusion.in_ref), custom_call_target="tpu_custom_call" | custom-call | tf_op jit(solution)/shard_map/ctx_exchange_1/pallas_call | solution.py:154
  192.2 6.8 copy.100
  199.0 6.7 reshape.510
  213.2 8.2 %ctx_exchange_2.1 = bf16[4,128,272]{2,1,0:T(8,128)(2,1)} custom-call(bf16[4,128,272]{2,1,0:T(8,128)(2,1)} %bitcast.253), custom_call_target="tpu_custom_call" | custom-call | tf_op jit(solution)/shard_map/ctx_exchange_2/pallas_call | solution.py:154
  224.7 17.4 %ctx_exchange_3.1 = bf16[4,128,1088]{2,1,0:T(8,128)(2,1)} custom-call(bf16[4,128,1088]{2,1,0:T(8,128)(2,1)} %bitcast.231), custom_call_target="tpu_custom_call" | custom-call | tf_op jit(solution)/shard_map/ctx_exchange_3/pallas_call | solution.py:154
  246.0 20.1 %ctx_exchange_4.1 = bf16[4,2,128,1088]{3,2,1,0:T(8,128)(2,1)} custom-call(bf16[2,128,1088]{2,1,0:T(8,128)(2,1)} %pad_maximum_fusion.2.in_ref), custom_call_target="tpu_custom_call" | custom-call | tf_op jit(solution)/shard_map/ctx_exchange_4/pallas_call | solution.py:154
  276.4 5.2 convolution_add_fusion
  281.6 5.4 fusion.52
  296.1 30.5 %ctx_exchange_5.1 = bf16[4,2,128,1088]{3,2,1,0:T(8,128)(2,1)} custom-call(bf16[4,2,128,1088]{3,2,1,0:T(8,128)(2,1)} %pad_maximum_fusion.in_ref), custom_call_target="tpu_custom_call" | custom-call | tf_op jit(solution)/shard_map/ctx_exchange_5/pallas_call | solution.py:154
  330.1 12.9 %ctx_exchange_6.1 = bf16[4,128,1088]{2,1,0:T(8,128)(2,1)} custom-call(bf16[128,1088]{1,0:T(8,128)(2,1)} %get-tuple-element.79.in_ref), custom_call_target="tpu_custom_call" | custom-call | tf_op jit(solution)/shard_map/ctx_exchange_6/pallas_call | solution.py:154
  345.9 8.1 %ctx_exchange_7.1 = bf16[4,128,272]{2,1,0:T(8,128)(2,1)} custom-call(bf16[4,128,272]{2,1,0:T(8,128)(2,1)} %bitcast.251), custom_call_target="tpu_custom_call" | custom-call | tf_op jit(solution)/shard_map/ctx_exchange_7/pallas_call | solution.py:154
  381.0 30.8 %ctx_exchange_8.1 = bf16[4,2,128,1088]{3,2,1,0:T(8,128)(2,1)} custom-call(bf16[4,2,128,1088]{3,2,1,0:T(8,128)(2,1)} %pad_maximum_fusion.1.in_ref), custom_call_target="tpu_custom_call" | custom-call | tf_op jit(solution)/shard_map/ctx_exchange_8/pallas_call | solution.py:154
  421.3 14.4 %ctx_exchange_9.1 = bf16[4,128,816]{2,1,0:T(8,128)(2,1)} custom-call(bf16[4,128,816]{2,1,0:T(8,128)(2,1)} %bitcast.239), custom_call_target="tpu_custom_call" | custom-call | tf_op jit(solution)/shard_map/ctx_exchange_9/pallas_call | solution.py:154
  455.0 4.8 convolution_convert_fusion
  465.4 17.5 %ctx_exchange_10.1 = bf16[4,128,1088]{2,1,0:T(8,128)(2,1)} custom-call(bf16[4,128,1088]{2,1,0:T(8,128)(2,1)} %bitcast.232), custom_call_target="tpu_custom_call" | custom-call | tf_op jit(solution)/shard_map/ctx_exchange_10/pallas_call | solution.py:154
  489.6 7.3 ctx_exchange_11.1
  498.7 33.4 %all-reduce.1 = f32[8,1632]{1,0:T(8,128)S(1)} all-reduce(f32[8,1632]{1,0:T(8,128)S(1)} %reduce_sum.235), channel_id=5, replica_groups=mesh['dp'=8,'ctx'=4] {'dp'}, use_global_device_ids=true, to_apply=%region_24.25.clone | all-reduce | flops 13056 | bytes 104448
  536.4 42.0 %reduce-scatter.13.cloned.1.call-done = bf16[136,272]{1,0:T(8,128)(2,1)} async-done(((bf16[1088,272]{1,0:T(8,128)(2,1)}), bf16[136,272]{1,0:T(8,128)(2,1)}) %reduce-scatter.13.cloned.1.call-update) | async-done | bytes 74000
  580.8 73.6 %reduce-scatter.11.cloned.1.call-done = bf16[1,272,544]{2,1,0:T(8,128)(2,1)} async-done(((bf16[8,272,544]{2,1,0:T(8,128)(2,1)}), bf16[1,272,544]{2,1,0:T(8,128)(2,1)}) %reduce-scatter.11.cloned.1.call-update) | async-done | bytes 295952 | tf_op jit(solution)/shard_map/reduce_scatter | solution.py:223
  656.1 76.8 %reduce-scatter.15.cloned.1.call-done = bf16[136,1088]{1,0:T(8,128)(2,1)} async-done(((bf16[1088,1088]{1,0:T(8,128)(2,1)}), bf16[136,1088]{1,0:T(8,128)(2,1)}) %reduce-scatter.15.cloned.1.call-update) | async-done | bytes 295952
  (197 shorter events, 146.2 us)
Async XLA Ops:
  7.2 92.2 %copy-start.21 = (bf16[1,128,1088]{1,2,0:T(8,128)(2,1)S(1)}, bf16[1,128,1088]{1,2,0:T(8,128)(2,1)}, u32[]{:S(2)}) copy-start(bf16[1,128,1088]{1,2,0:T(8,128)(2,1)} %param.27) | copy-start | bytes 835588
  7.2 93.1 %copy-start.23 = (bf16[272,136]{0,1:T(8,128)(2,1)S(1)}, bf16[272,136]{0,1:T(8,128)(2,1)}, u32[]{:S(2)}) copy-start(bf16[272,136]{0,1:T(8,128)(2,1)} %param.19) | copy-start | bytes 221956
  7.2 146.2 %all-gather.9.cloned.1.call-start = ((), (), s32[]{:S(2)}) async-start(), calls=%async_computation.7 | async-start | bytes 2506752 | tf_op jit(solution)/shard_map/all_gather | solution.py:214
  7.2 1.7 collective-permute-start
  9.7 259.7 %all-gather.11.cloned.1.call-start = ((), (), s32[]{:S(2)}) async-start(), calls=%async_computation.8 | async-start | bytes 3133440 | tf_op jit(solution)/shard_map/all_gather | solution.py:214
  9.8 1.6 collective-permute-start.1
  12.2 269.4 %all-gather.7.cloned.1.call-start = ((), (), s32[]{:S(2)}) async-start(), calls=%async_computation.4 | async-start | bytes 2820096 | tf_op jit(solution)/shard_map/all_gather | solution.py:227
  12.9 521.9 %reduce-scatter.9.cloned.1.call-start = ((), (), s32[]{:S(2)}) async-start(), calls=%async_computation.5 | async-start | bytes 2506752 | tf_op jit(solution)/shard_map/reduce_scatter | solution.py:223
  134.9 86.4 %copy-start.7 = (bf16[1088,272]{1,0:T(8,128)(2,1)}, bf16[1088,272]{1,0:T(8,128)(2,1)S(1)}, u32[]{:S(2)}) copy-start(bf16[1088,272]{1,0:T(8,128)(2,1)S(1)} %all_gather.28) | copy-start | bytes 1775620
  212.2 9.1 %copy-start.19 = (bf16[17,64,128]{2,1,0:T(8,128)(2,1)}, bf16[17,64,128]{2,1,0:T(8,128)(2,1)S(1)}, u32[]{:S(2)}) copy-start(bf16[17,64,128]{2,1,0:T(8,128)(2,1)S(1)} %convolution_convert_fusion.10) | copy-start | bytes 835588
  281.6 5.4 copy-start.12
  281.6 5.5 copy-start.13
  287.0 3.2 copy-start.14
  287.0 3.1 copy-start.25
  287.1 3.1 copy-start.24
  328.8 14.3 %copy-start.8 = (bf16[1088,272]{1,0:T(8,128)(2,1)S(1)}, bf16[1088,272]{1,0:T(8,128)(2,1)}, u32[]{:S(2)}) copy-start(bf16[1088,272]{1,0:T(8,128)(2,1)} %copy-done.7) | copy-start | bytes 1775620
  356.3 3.7 copy-start.17
  359.9 3.7 copy-start.2
  442.1 136.2 %reduce-scatter.13.cloned.1.call-start = ((), (), s32[]{:S(2)}) async-start(), calls=%async_computation.9 | async-start | bytes 940032
  446.1 208.4 %reduce-scatter.11.cloned.1.call-start = ((), (), s32[]{:S(2)}) async-start(), calls=%async_computation.6 | async-start | bytes 3133440 | tf_op jit(solution)/shard_map/reduce_scatter | solution.py:223
  455.0 277.9 %reduce-scatter.15.cloned.1.call-start = ((), (), s32[]{:S(2)}) async-start(), calls=%async_computation.10 | async-start | bytes 2820096
  465.4 19.7 %copy-start.4 = (f32[128,1088]{1,0:T(8,128)S(1)}, f32[128,1088]{1,0:T(8,128)}, u32[]{:S(2)}) copy-start(f32[128,1088]{1,0:T(8,128)} %copy-done.3) | copy-start | bytes 1671172
  534.8 45.2 %collective-permute-start.2 = (bf16[272,408]{1,0:T(8,128)(2,1)}, bf16[272,408]{1,0:T(8,128)(2,1)S(1)}, u32[]{:S(2)}, u32[]{:S(2)}) collective-permute-start(bf16[272,408]{1,0:T(8,128)(2,1)} %bitcast.273), channel_id=1, source_target_pairs={{0,0},{8,1},{16,2},{24,3},{4,4},{12,5},{20,6},{28,7},{1,8},{9,9},{... | collective-permute-start | bytes 665864 | tf_op jit(solution)/shard_map/ppermute | solution.py:224
  654.5 80.3 %collective-permute-start.3 = (bf16[272,544]{1,0:T(8,128)(2,1)}, bf16[272,544]{1,0:T(8,128)(2,1)S(1)}, u32[]{:S(2)}, u32[]{:S(2)}) collective-permute-start(bf16[272,544]{1,0:T(8,128)(2,1)} %bitcast.272), channel_id=1, source_target_pairs={{0,0},{8,1},{16,2},{24,3},{4,4},{12,5},{20,6},{28,7},{1,8},{9,9},{... | collective-permute-start | bytes 887816 | tf_op jit(solution)/shard_map/ppermute | solution.py:224
  (13 other events, 20.7 us)
Sparse Core Ops, SparseCore 0:
  10.8 70.7 all-gather.8
  84.3 62.4 all-gather.10
  149.0 52.4 all-gather.6
  442.2 67.0 reduce-scatter.8
  512.6 65.7 reduce-scatter.12
  581.7 72.6 reduce-scatter.10
  658.1 74.7 reduce-scatter.14

commit v2 on v1

--- a/solution.py
+++ b/solution.py
@@ -173,6 +173,64 @@
     count = lax.axis_size("ctx")
     kernel = relay_kernel if count == 4 else share_kernel
     return ctx_call(kernel, block, (count,) + block.shape, ident)
+
+
+def owners_kernel(count, *refs):
+    arrays = (len(refs) - 2) // 2
+    sources, results = refs[:arrays], refs[arrays : 2 * arrays]
+    send_sem, recv_sem = refs[2 * arrays :]
+    me = lax.axis_index("dp")
+    barrier = pltpu.get_barrier_semaphore()
+    for step in range(1, count):
+        pl.semaphore_signal(
+            barrier,
+            inc=1,
+            device_id={"dp": lax.rem(me + step, count)},
+            device_id_type=pl.DeviceIdType.MESH,
+        )
+    pl.semaphore_wait(barrier, count - 1)
+
+    def copy_of(step, which):
+        target = lax.rem(me + step, count)
+        return pltpu.make_async_remote_copy(
+            src_ref=sources[which].at[target],
+            dst_ref=results[which].at[me],
+            send_sem=send_sem.at[which, step],
+            recv_sem=recv_sem.at[which, step],
+            device_id={"dp": target},
+            device_id_type=pl.DeviceIdType.MESH,
+        )
+
+    def start(step, carry):
+        for which in range(arrays):
+            copy_of(step, which).start()
+        return carry
+
+    def finish(step, carry):
+        for which in range(arrays):
+            copy_of(step, which).wait()
+        return carry
+
+    lax.fori_loop(1, count, start, 0)
+    for which in range(arrays):
+        results[which][pl.ds(me, 1)] = sources[which][pl.ds(me, 1)]
+    lax.fori_loop(1, count, finish, 0)
+
+
+def to_owners(arrays, ident):
+    count = lax.axis_size("dp")
+    return pl.pallas_call(
+        functools.partial(owners_kernel, count),
+        out_shape=[jax.ShapeDtypeStruct(a.shape, a.dtype) for a in arrays],
+        in_specs=[pl.BlockSpec(memory_space=pltpu.VMEM)] * len(arrays),
+        out_specs=[pl.BlockSpec(memory_space=pltpu.VMEM)] * len(arrays),
+        scratch_shapes=[
+            pltpu.SemaphoreType.DMA((len(arrays), count)),
+            pltpu.SemaphoreType.DMA((len(arrays), count)),
+        ],
+        compiler_params=pltpu.CompilerParams(collective_id=ident, has_side_effects=True),
+        name=f"dp_owners_{ident}",
+    )(*arrays)
 
 
 def on_device(
@@ -209,26 +267,24 @@
             there.append((d * ctx + c, (fold * c + d % fold) * ctx + d // fold))
     back = [(b, a) for a, b in there]
 
+    def columns_joined(whole):
+        high, wide = whole.shape[1:]
+        whole = whole.reshape(ctx, fold, high, wide)
+        return whole.transpose(0, 2, 1, 3).reshape(ctx * high, fold * wide)
+
     def columns_whole(piece):
         moved = lax.ppermute(piece, ("dp", "ctx"), there)
-        whole = lax.all_gather(moved, "dp", axis=0, tiled=False)
-        whole = whole.reshape(ctx, fold, piece.shape[0], piece.shape[1])
-        return whole.transpose(0, 2, 1, 3).reshape(
-            ctx * piece.shape[0], fold * piece.shape[1]
-        )
-
-    def columns_owned(part, piece):
+        return columns_joined(lax.all_gather(moved, "dp", axis=0, tiled=False))
+
+    def columns_split(part, piece):
         parts = part.reshape(ctx, piece.shape[0], fold, piece.shape[1]).transpose(0, 2, 1, 3)
-        parts = parts.reshape(dp, piece.shape[0], piece.shape[1]).astype(low)
-        mine = lax.psum_scatter(parts, "dp", scatter_dimension=0, tiled=False)
-        return lax.ppermute(mine, ("dp", "ctx"), back).astype(jnp.float32) * grad_scale
+        return parts.reshape(dp, piece.shape[0], piece.shape[1]).astype(low)
+
+    def columns_back(mine):
+        return lax.ppermute(mine.astype(low), ("dp", "ctx"), back).astype(jnp.float32) * grad_scale
 
     def rows_whole(piece):
         return lax.all_gather(piece.T, "dp", axis=0, tiled=True)
-
-    def rows_owned(part):
-        mine = lax.psum_scatter(part.astype(low), "dp", scatter_dimension=0, tiled=True)
-        return mine.T.astype(jnp.float32) * grad_scale
 
     shards = (
         norm_one_gain,
@@ -241,7 +297,15 @@
         bias_down,
     )
     sizes = [v.shape[0] for v in shards]
-    vectors = lax.all_gather(jnp.concatenate(shards), "dp", axis=0, tiled=False)
+    lanes = w_qkv.shape[1] + w_out.shape[1]
+    packed = jnp.concatenate(shards)
+    used = packed.shape[0]
+    packed = jnp.pad(packed, (0, -used % lanes)).reshape(-1, lanes)
+    moved_qkv = lax.ppermute(w_qkv, ("dp", "ctx"), there)
+    first = jnp.concatenate([jnp.concatenate([moved_qkv, w_out], axis=1), packed], axis=0)
+    first = lax.all_gather(first, "dp", axis=0, tiled=False)
+    part_rows, part_cols = w_qkv.shape
+    vectors = first[:, part_rows:].reshape(dp, -1)[:, :used]
     full = []
     at = 0
     for size in sizes:
@@ -258,14 +322,20 @@
         full_bias_down,
     ) = full
 
-    qkv_c = columns_whole(w_qkv)
-    out_c = rows_whole(w_out)
+    qkv_c = columns_joined(first[:, :part_rows, :part_cols])
+    out_c = (
+        first[:, :part_rows, part_cols:].transpose(1, 0, 2).reshape(part_rows, dp * w_out.shape[1])
+    )
     up_c = columns_whole(w_up)
     down_c = rows_whole(w_down)
 
     inputs = block_input.reshape(rows, width).astype(jnp.float32)
-    scaled_one, inverse_one, normed_one = norm_forward(inputs, gain_one, shift_one)
-    normed_one_all = ctx_share(normed_one, 0).reshape(tokens, width)
+    scaled_one, inverse_one, _ = norm_forward(inputs, gain_one, shift_one)
+    upstream = cotangent.reshape(rows, width)
+    both = ctx_share(jnp.stack([block_input.reshape(rows, width), upstream]), 0)
+    upstream_all = both[:, 1].reshape(tokens, width)
+    inputs_all = both[:, 0].reshape(tokens, width).astype(jnp.float32)
+    normed_one_all = norm_forward(inputs_all, gain_one, shift_one)[2]
     qkv_bias = jnp.concatenate(
         [full_bias_qv[:width], jnp.zeros((width,), jnp.float32), full_bias_qv[width:]]
     )
@@ -304,15 +374,12 @@
         return swapped
 
     mixed_c = ctx_swap(to_columns(mixed.reshape(rows, width)), 2).reshape(tokens, slab)
-    out_part = outer_cols(mixed_c, out_c).astype(low).reshape(ctx, rows, width)
+    out_part = jnp.dot(mixed_c, out_c, preferred_element_type=jnp.float32).astype(low).reshape(ctx, rows, width)
     out_sum = jnp.sum(ctx_swap(out_part, 3).astype(jnp.float32), axis=0)
     residual = inputs + (out_sum + full_bias_out)
     scaled_two, inverse_two, normed_two = norm_forward(residual, gain_two, shift_two)
-    upstream = cotangent.reshape(rows, width)
     up_float = upstream.astype(jnp.float32)
-    both = ctx_share(jnp.stack([normed_two, upstream]), 4)
-    normed_two_all = both[:, 0].reshape(tokens, width)
-    upstream_all = both[:, 1].reshape(tokens, width)
+    normed_two_all = ctx_share(normed_two, 4).reshape(tokens, width)
     units = up_c.shape[1]
     hidden_pre = jnp.dot(
         normed_two_all, up_c, preferred_element_type=jnp.float32
@@ -327,6 +394,11 @@
     sums = jnp.sum(
         ctx_swap(jnp.stack([down_part, normed_part], axis=1), 5).astype(jnp.float32), axis=0
     )
+    down_grad = inner_rows(upstream_all, hidden).astype(low)
+    up_grad = columns_split(inner_rows(normed_two_all, grad_hidden_low), w_up)
+    down_grad, up_grad, sums = lax.optimization_barrier((down_grad, up_grad, sums))
+    down_mine = lax.psum_scatter(down_grad, "dp", scatter_dimension=0, tiled=True)
+    up_mine = lax.psum_scatter(up_grad, "dp", scatter_dimension=0, tiled=False)
     block_output = (
         (residual + (sums[0] + full_bias_down)).astype(low).reshape(seq_count, block_len, width)
     )
@@ -334,9 +406,7 @@
     grad_residual = up_float + norm_backward(grad_normed_two, scaled_two, inverse_two, gain_two)
     grad_residual_low = grad_residual.astype(low)
     grad_residual_all = ctx_share(grad_residual_low, 6).reshape(tokens, width)
-    grad_mixed_c = jnp.dot(
-        grad_residual_all, out_c, preferred_element_type=jnp.float32
-    ).astype(low)
+    grad_mixed_c = outer_cols(grad_residual_all, out_c).astype(low)
     grad_mixed = ctx_swap(grad_mixed_c.reshape(ctx, rows, slab), 7)
     grad_mixed = grad_mixed.transpose(1, 0, 2).reshape(seq_count, block_len, HEADS, HEAD_DIM)
     grad_probs = jnp.einsum(
@@ -370,10 +440,12 @@
     grad_input = grad_residual + norm_backward(grad_normed_one, scaled_one, inverse_one, gain_one)
     grad_input = grad_input.reshape(seq_count, block_len, width)
 
-    grad_down = rows_owned(inner_rows(upstream_all, hidden))
-    grad_up = columns_owned(inner_rows(normed_two_all, grad_hidden_low), w_up)
-    grad_out = rows_owned(inner_rows(grad_residual_all, mixed_c))
-    grad_qkv = columns_owned(inner_rows(normed_one_all, grad_projected_c), w_qkv)
+    grad_down = down_mine.T.astype(jnp.float32) * grad_scale
+    grad_up = columns_back(up_mine)
+    qkv_parts = columns_split(inner_rows(normed_one_all, grad_projected_c), w_qkv)
+    out_parts = (
+        inner_rows(grad_residual_all, mixed_c).astype(low).reshape(dp, w_out.shape[1], slab)
+    )
 
     bias_up_c = jnp.sum(grad_hidden, axis=0)
     grad_bias_up = lax.dynamic_update_slice_in_dim(
@@ -391,7 +463,10 @@
     )
     table = jnp.concatenate([v.reshape(dp, -1) for v in sums_here], axis=1)
     table = jnp.sum(ctx_share(table, 11), axis=0)
-    totals = lax.psum_scatter(table, "dp", scatter_dimension=0, tiled=False) * grad_scale
+    qkv_parts, out_parts, table = to_owners([qkv_parts, out_parts, table[:, None]], 12)
+    grad_qkv = columns_back(jnp.sum(qkv_parts.astype(jnp.float32), axis=0))
+    grad_out = jnp.sum(out_parts.astype(jnp.float32), axis=0).T * grad_scale
+    totals = jnp.sum(table, axis=(0, 1)) * grad_scale
     owned = []
     at = 0
     for size in sizes:

time: 754 us -> 599 us (0.79)
  the two profiles are of different devices: /device:TPU:0 before, /device:TPU:19 now
where the time goes in v2:
time: 599 us; the launch traced here: 590 us
  Pallas kernels  282 us (47%)
  local copies, waits for them, and re-layouts  118 us (20%)
  waiting for transfers between devices  57.7 us (10%)
  matrix products  56.9 us (9%)
  other arithmetic  44.4 us (7%)
  starting transfers between devices  16.1 us (3%)
  between operations  14.7 us (2%)
    pallas_call x12, Pallas kernels, ctx_call(): pl.pallas_call(functools.partial(kernel, count), out_shape=jax.ShapeDtype...  210 us
    pallas_call x1, Pallas kernels, to_owners(): pl.pallas_call(functools.partial(owners_kernel, count), out_shape=[jax.Sh...  72 us
    ppermute x1, waiting for transfers between devices, columns_whole(): moved = lax.ppermute(piece, ('dp', 'ctx'), there)  26.6 us
    ppermute x2, waiting for transfers between devices, columns_back(): lax.ppermute(mine.astype(low), ('dp', 'ctx'), back).astype(jnp.float32)  21.7 us
    dot_general x4, matrix products, outer_cols(): lax.dot_general(left, right, (((1,), (1,)), ((), ())), preferred_element_...  13.8 us
    reshape x2, local copies, waits for them, and re-layouts, columns_joined(): return whole.transpose(0, 2, 1, 3).reshape(ctx * high, fold * wide)  12.7 us
  transfers between devices with their start and end apart: 9, of which 5 were waited for; matrix products, arithmetic and copies ran while one was open for 30% of the time, Pallas kernels for 43%

profile of v2, /device:TPU:19, one launch (start us, length us, event | category | flops | bytes accessed | tf_op | source)
XLA Modules:
  0.0 590.0 jit_solution(10925684899882804246)
XLA Ops:
  17.5 7.3 %collective-permute-done = bf16[272,408]{1,0:T(8,128)(2,1)S(1)} collective-permute-done((bf16[272,408]{1,0:T(8,128)(2,1)}, bf16[272,408]{1,0:T(8,128)(2,1)S(1)}, u32[]{:S(2)}, u32[]{:S(2)}) %collective-permute-start) | collective-permute-done | bytes 221984 | tf_op jit(solution)/shard_map/ppermute | solution.py:304
  29.4 26.6 %collective-permute-done.1 = bf16[272,544]{1,0:T(8,128)(2,1)S(1)} collective-permute-done((bf16[272,544]{1,0:T(8,128)(2,1)}, bf16[272,544]{1,0:T(8,128)(2,1)S(1)}, u32[]{:S(2)}, u32[]{:S(2)}) %collective-permute-start.1) | collective-permute-done | bytes 295968 | tf_op jit(solution)/shard_map/ppermute | solution.py:276
  59.0 19.8 %ctx_exchange_0.1 = bf16[4,2,128,1088]{3,2,1,0:T(8,128)(2,1)} custom-call(bf16[2,128,1088]{2,1,0:T(8,128)(2,1)} %pad_maximum_fusion.2.in_ref), custom_call_target="tpu_custom_call" | custom-call | tf_op jit(solution)/shard_map/ctx_exchange_0/pallas_call | solution.py:154
  96.3 6.2 %reshape.543 = bf16[1088,816]{1,0:T(8,128)(2,1)} reshape(bf16[4,272,2,408]{3,2,1,0:T(2,128)(2,1)} %bitcast.230) | data formatting | bytes 3551232 | tf_op jit(solution)/shard_map/reshape | solution.py:273
  106.5 29.1 %ctx_exchange_1.1 = bf16[4,512,816]{2,1,0:T(8,128)(2,1)} custom-call(bf16[512,816]{1,0:T(8,128)(2,1)} %add_convert_fusion.1.in_ref), custom_call_target="tpu_custom_call" | custom-call | tf_op jit(solution)/shard_map/ctx_exchange_1/pallas_call | solution.py:154
  135.6 6.8 %copy.114 = bf16[4,4,1,128,816]{3,1,4,0,2:T(4,128)(2,1)} copy(bf16[4,4,1,128,816]{4,3,1,0,2:T(8,128)(2,1)} %bitcast.224) | data formatting | bytes 6684672 | tf_op jit(solution)/shard_map/reshape | solution.py:349
  142.3 6.7 %reshape.545 = bf16[1,512,3264]{1,2,0:T(8,128)(2,1)} reshape(bf16[1,4,128,4,816]{2,1,4,3,0:T(4,128)(2,1)} %bitcast.225) | data formatting | bytes 6684672 | tf_op jit(solution)/shard_map/reshape | solution.py:351
  165.4 8.5 %ctx_exchange_2.1 = bf16[4,128,272]{2,1,0:T(8,128)(2,1)} custom-call(bf16[4,128,272]{2,1,0:T(8,128)(2,1)} %bitcast.257), custom_call_target="tpu_custom_call" | custom-call | tf_op jit(solution)/shard_map/ctx_exchange_2/pallas_call | solution.py:154
  179.3 17.9 %ctx_exchange_3.1 = bf16[4,128,1088]{2,1,0:T(8,128)(2,1)} custom-call(bf16[4,128,1088]{2,1,0:T(8,128)(2,1)} %bitcast.237), custom_call_target="tpu_custom_call" | custom-call | tf_op jit(solution)/shard_map/ctx_exchange_3/pallas_call | solution.py:154
  202.9 12.5 %ctx_exchange_4.1 = bf16[4,128,1088]{2,1,0:T(8,128)(2,1)} custom-call(bf16[128,1088]{1,0:T(8,128)(2,1)} %add_convert_fusion.3.in_ref), custom_call_target="tpu_custom_call" | custom-call | tf_op jit(solution)/shard_map/ctx_exchange_4/pallas_call | solution.py:154
  219.6 5.5 copy.152
  225.1 6.6 %reshape.554 = bf16[1088,1088]{1,0:T(8,128)(2,1)} reshape(bf16[4,272,2,544]{3,2,1,0:T(2,128)(2,1)} %bitcast.226) | data formatting | bytes 4734976 | tf_op jit(solution)/shard_map/reshape | solution.py:273
  236.7 6.0 %fusion.53 = (f32[1088]{0:T(1024)}, bf16[512,1088]{0,1:T(8,128)(2,1)S(1)}, f32[512,1088]{0,1:T(8,128)S(1)}) fusion(f32[512,1088]{0,1:T(8,128)} %convolution_add_fusion, bf16[512,1088]{1,0:T(8,128)(2,1)} %bitcast.258, bf16[1088,1088]{1,0:T(8,128)(2,1)} %all-gather.7.cloned.1.call-done), kind=kOutput, calls=%fused_computation.142 | convolution fusion | flops 1219394560 | bytes 9056512 | tf_op jit(solution)/shard_map/dot_general | solution.py:389
  263.7 30.8 %ctx_exchange_5.1 = bf16[4,2,128,1088]{3,2,1,0:T(8,128)(2,1)} custom-call(bf16[4,2,128,1088]{3,2,1,0:T(8,128)(2,1)} %pad_maximum_fusion.in_ref), custom_call_target="tpu_custom_call" | custom-call | tf_op jit(solution)/shard_map/ctx_exchange_5/pallas_call | solution.py:154
  310.9 12.6 %ctx_exchange_6.1 = bf16[4,128,1088]{2,1,0:T(8,128)(2,1)} custom-call(bf16[128,1088]{1,0:T(8,128)(2,1)} %get-tuple-element.91.in_ref), custom_call_target="tpu_custom_call" | custom-call | tf_op jit(solution)/shard_map/ctx_exchange_6/pallas_call | solution.py:154
  328.3 8.6 %ctx_exchange_7.1 = bf16[4,128,272]{2,1,0:T(8,128)(2,1)} custom-call(bf16[4,128,272]{2,1,0:T(8,128)(2,1)} %bitcast.255), custom_call_target="tpu_custom_call" | custom-call | tf_op jit(solution)/shard_map/ctx_exchange_7/pallas_call | solution.py:154
  371.6 31.4 %ctx_exchange_8.1 = bf16[4,2,128,1088]{3,2,1,0:T(8,128)(2,1)} custom-call(bf16[4,2,128,1088]{3,2,1,0:T(8,128)(2,1)} %pad_maximum_fusion.1.in_ref), custom_call_target="tpu_custom_call" | custom-call | tf_op jit(solution)/shard_map/ctx_exchange_8/pallas_call | solution.py:154
  410.1 14.4 %ctx_exchange_9.1 = bf16[4,128,816]{2,1,0:T(8,128)(2,1)} custom-call(bf16[4,128,816]{2,1,0:T(8,128)(2,1)} %bitcast.243), custom_call_target="tpu_custom_call" | custom-call | tf_op jit(solution)/shard_map/ctx_exchange_9/pallas_call | solution.py:154
  429.3 17.9 %ctx_exchange_10.1 = bf16[4,128,1088]{2,1,0:T(8,128)(2,1)} custom-call(bf16[4,128,1088]{2,1,0:T(8,128)(2,1)} %bitcast.238), custom_call_target="tpu_custom_call" | custom-call | tf_op jit(solution)/shard_map/ctx_exchange_10/pallas_call | solution.py:154
  457.1 6.7 %ctx_exchange_11.1 = f32[4,8,1632]{2,1,0:T(8,128)} custom-call(f32[8,1632]{1,0:T(8,128)} %concatenate.35.in_ref), custom_call_target="tpu_custom_call" | custom-call | tf_op jit(solution)/shard_map/ctx_exchange_11/pallas_call | solution.py:154
  469.5 72.0 %dp_owners_12.1 = (bf16[8,272,408]{2,1,0:T(8,128)(2,1)}, bf16[8,136,272]{2,1,0:T(8,128)(2,1)}, f32[8,1,1632]{2,1,0:T(1,128)}) custom-call(bf16[8,272,408]{2,1,0:T(8,128)(2,1)} %bitcast.254, bf16[8,136,272]{2,1,0:T(8,128)(2,1)} %bitcast.245, f32[8,1,1632]{2,1,0:T(1,128)} %broadcast_in_dim.18.refs_2_), custom_call_target="tpu_custom_call" | custom-call | tf_op jit(solution)/shard_map/dp_owners_12/pallas_call | solution.py:222
  547.8 6.7 %collective-permute-start.2 = (bf16[272,408]{1,0:T(8,128)(2,1)S(1)}, bf16[272,408]{1,0:T(8,128)(2,1)S(1)}, u32[]{:S(2)}, u32[]{:S(2)}) collective-permute-start(bf16[272,408]{1,0:T(8,128)(2,1)S(1)} %reduce_sum.287), channel_id=1, source_target_pairs={{0,0},{8,1},{16,2},{24,3},{4,4},{12,5},{20,6},{28,7},{1,8},{9,9},{... | collective-permute-start | bytes 665864 | tf_op jit(solution)/shard_map/ppermute | solution.py:284
  556.0 11.4 %collective-permute-done.2 = bf16[272,408]{1,0:T(8,128)(2,1)S(1)} collective-permute-done((bf16[272,408]{1,0:T(8,128)(2,1)S(1)}, bf16[272,408]{1,0:T(8,128)(2,1)S(1)}, u32[]{:S(2)}, u32[]{:S(2)}) %collective-permute-start.2) | collective-permute-done | bytes 221984 | tf_op jit(solution)/shard_map/ppermute | solution.py:284
  572.0 10.3 %collective-permute-done.3 = bf16[272,544]{1,0:T(8,128)(2,1)S(1)} collective-permute-done((bf16[272,544]{1,0:T(8,128)(2,1)}, bf16[272,544]{1,0:T(8,128)(2,1)S(1)}, u32[]{:S(2)}, u32[]{:S(2)}) %collective-permute-start.3) | collective-permute-done | bytes 295968 | tf_op jit(solution)/shard_map/ppermute | solution.py:284
  (236 shorter events, 193.2 us)
Async XLA Ops:
  7.2 50.3 %copy-start.27 = (bf16[1,128,1088]{1,2,0:T(8,128)(2,1)S(1)}, bf16[1,128,1088]{1,2,0:T(8,128)(2,1)}, u32[]{:S(2)}) copy-start(bf16[1,128,1088]{1,2,0:T(8,128)(2,1)} %param.14) | copy-start | bytes 835588
  7.2 50.7 %copy-start.28 = (bf16[1,128,1088]{1,2,0:T(8,128)(2,1)S(1)}, bf16[1,128,1088]{1,2,0:T(8,128)(2,1)}, u32[]{:S(2)}) copy-start(bf16[1,128,1088]{1,2,0:T(8,128)(2,1)} %param.27) | copy-start | bytes 835588
  7.2 79.3 %all-gather.11.cloned.1.call-start = ((), (), s32[]{:S(2)}) async-start(), calls=%async_computation.5 | async-start | bytes 3225600 | tf_op jit(solution)/shard_map/all_gather | solution.py:306
  7.2 17.6 %collective-permute-start = (bf16[272,408]{1,0:T(8,128)(2,1)}, bf16[272,408]{1,0:T(8,128)(2,1)S(1)}, u32[]{:S(2)}, u32[]{:S(2)}) collective-permute-start(bf16[272,408]{1,0:T(8,128)(2,1)} %param.17), channel_id=1, source_target_pairs={{0,0},{1,8},{2,16},{3,24},{4,4},{5,12},{6,20},{7,28},{8,1},{9,9},{... | collective-permute-start | bytes 665864 | tf_op jit(solution)/shard_map/ppermute | solution.py:304
  25.7 193.8 %all-gather.9.cloned.1.call-start = ((), (), s32[]{:S(2)}) async-start(), calls=%async_computation.4 | async-start | bytes 3133440 | tf_op jit(solution)/shard_map/all_gather | solution.py:277
  25.8 30.2 %collective-permute-start.1 = (bf16[272,544]{1,0:T(8,128)(2,1)}, bf16[272,544]{1,0:T(8,128)(2,1)S(1)}, u32[]{:S(2)}, u32[]{:S(2)}) collective-permute-start(bf16[272,544]{1,0:T(8,128)(2,1)} %param.23), channel_id=1, source_target_pairs={{0,0},{1,8},{2,16},{3,24},{4,4},{5,12},{6,20},{7,28},{8,1},{9,9},{... | collective-permute-start | bytes 887816 | tf_op jit(solution)/shard_map/ppermute | solution.py:276
  56.7 180.0 %all-gather.7.cloned.1.call-start = ((), (), s32[]{:S(2)}) async-start(), calls=%async_computation.2 | async-start | bytes 2820096 | tf_op jit(solution)/shard_map/all_gather | solution.py:287
  57.5 510.7 %reduce-scatter.5.cloned.1.call-start = ((), (), s32[]{:S(2)}) async-start(), calls=%async_computation.3 | async-start | bytes 3133440 | tf_op jit(solution)/shard_map/reduce_scatter | solution.py:401
  83.0 79.4 %copy-start.22 = (pred[128,512]{1,0:T(8,128)(4,1)}, pred[128,512]{1,0:T(8,128)(4,1)S(1)}, u32[]{:S(2)}) copy-start(pred[128,512]{1,0:T(8,128)(4,1)S(1)} %iota_compare_fusion) | copy-start | bytes 196612
  90.1 12.5 %copy-start.29 = (f32[1088]{0:T(1024)}, f32[1088]{0:T(1024)S(1)}, u32[]{:S(2)}) copy-start(f32[1088]{0:T(1024)S(1)} %reshape.571) | copy-start | bytes 13060
  164.5 14.9 %copy-start.21 = (bf16[17,64,128]{2,1,0:T(8,128)(2,1)}, bf16[17,64,128]{2,1,0:T(8,128)(2,1)S(1)}, u32[]{:S(2)}) copy-start(bf16[17,64,128]{2,1,0:T(8,128)(2,1)S(1)} %convolution_convert_fusion.10) | copy-start | bytes 835588
  236.7 6.0 %copy-start.12 = (bf16[1088,1088]{1,0:T(8,128)(2,1)S(1)}, bf16[1088,1088]{1,0:T(8,128)(2,1)}, u32[]{:S(2)}) copy-start(bf16[1088,1088]{1,0:T(8,128)(2,1)} %reshape.554) | copy-start | bytes 7102468
  236.7 6.0 %copy-start.13 = (f32[512,1088]{0,1:T(8,128)S(1)}, f32[512,1088]{0,1:T(8,128)}, u32[]{:S(2)}) copy-start(f32[512,1088]{0,1:T(8,128)} %convolution_add_fusion) | copy-start | bytes 6684676
  301.2 269.0 %reduce-scatter.7.cloned.1.call-start = ((), (), s32[]{:S(2)}) async-start(), calls=%async_computation.6 | async-start | bytes 2820096
  323.5 15.3 %copy-start.3 = (bf16[4,128,1088]{2,1,0:T(8,128)(2,1)S(1)}, bf16[4,128,1088]{2,1,0:T(8,128)(2,1)}, u32[]{:S(2)}) copy-start(bf16[4,128,1088]{2,1,0:T(8,128)(2,1)} %ctx_exchange_6.1) | copy-start | bytes 3342340
  323.5 15.3 %copy-start.8 = (bf16[4,128,272]{2,1,0:T(8,128)(2,1)S(1)}, bf16[4,128,272]{2,1,0:T(8,128)(2,1)}, u32[]{:S(2)}) copy-start(bf16[4,128,272]{2,1,0:T(8,128)(2,1)} %ctx_exchange_2.1) | copy-start | bytes 835588
  429.3 20.3 %copy-start.38 = (f32[128]{0:T(128)S(1)}, f32[128]{0:T(128)}, u32[]{:S(2)}) copy-start(f32[128]{0:T(128)} %broadcast_multiply_fusion.4) | copy-start | bytes 1540
  429.3 20.3 %copy-start.39 = (f32[128]{0:T(128)S(1)}, f32[128]{0:T(128)}, u32[]{:S(2)}) copy-start(f32[128]{0:T(128)} %get-tuple-element.130) | copy-start | bytes 1540
  429.3 21.3 %copy-start.7 = (f32[128,1088]{1,0:T(8,128)S(1)}, f32[128,1088]{1,0:T(8,128)}, u32[]{:S(2)}) copy-start(f32[128,1088]{1,0:T(8,128)} %copy-done.6) | copy-start | bytes 1671172
  453.2 13.6 %copy-start.18 = (bf16[1088,512]{1,0:T(8,128)(2,1)S(1)}, bf16[1088,512]{1,0:T(8,128)(2,1)}, u32[]{:S(2)}) copy-start(bf16[1088,512]{1,0:T(8,128)(2,1)} %copy.131) | copy-start | bytes 3342340
  469.5 75.3 %copy-start.15 = (bf16[1,128,1088]{2,1,0:T(8,128)(2,1)S(1)}, bf16[1,128,1088]{2,1,0:T(8,128)(2,1)}, u32[]{:S(2)}) copy-start(bf16[1,128,1088]{2,1,0:T(8,128)(2,1)} %get-tuple-element.100) | copy-start | bytes 835588
  541.6 12.9 %copy-start.25 = (bf16[8,136,272]{2,1,0:T(8,128)(2,1)S(1)}, bf16[8,136,272]{2,1,0:T(8,128)(2,1)}, u32[]{:S(2)}) copy-start(bf16[8,136,272]{2,1,0:T(8,128)(2,1)} %get-tuple-element.23) | copy-start | bytes 1775620
  547.8 19.5 %collective-permute-start.2 = (bf16[272,408]{1,0:T(8,128)(2,1)S(1)}, bf16[272,408]{1,0:T(8,128)(2,1)S(1)}, u32[]{:S(2)}, u32[]{:S(2)}) collective-permute-start(bf16[272,408]{1,0:T(8,128)(2,1)S(1)} %reduce_sum.287), channel_id=1, source_target_pairs={{0,0},{8,1},{16,2},{24,3},{4,4},{12,5},{20,6},{28,7},{1,8},{9,9},{... | collective-permute-start | bytes 665864 | tf_op jit(solution)/shard_map/ppermute | solution.py:284
  568.2 14.1 %collective-permute-start.3 = (bf16[272,544]{1,0:T(8,128)(2,1)}, bf16[272,544]{1,0:T(8,128)(2,1)S(1)}, u32[]{:S(2)}, u32[]{:S(2)}) collective-permute-start(bf16[272,544]{1,0:T(8,128)(2,1)} %bitcast.270), channel_id=1, source_target_pairs={{0,0},{8,1},{16,2},{24,3},{4,4},{12,5},{20,6},{28,7},{1,8},{9,9},{... | collective-permute-start | bytes 887816 | tf_op jit(solution)/shard_map/ppermute | solution.py:284
  (28 other events, 79.2 us)
Sparse Core Ops, SparseCore 0:
  25.9 60.5 all-gather.10
  89.2 54.7 all-gather.8
  146.2 51.7 all-gather.6
  301.3 72.1 reduce-scatter.4
  377.0 70.0 reduce-scatter.6

commit v3 on v2

--- a/solution.py
+++ b/solution.py
@@ -127,38 +127,100 @@
     partner = me + 1 - 2 * lax.rem(me, 2)
     across = lax.rem(me + 2, 4)
 
-    def send(source, slot, sem, target):
+    chunks = send_sem.shape[1]
+    size = in_ref.shape[0] // chunks
+
+    def send(source, slot, sem, part, target):
         copy = pltpu.make_async_remote_copy(
             src_ref=source,
-            dst_ref=out_ref.at[slot],
-            send_sem=send_sem.at[sem],
-            recv_sem=recv_sem.at[sem],
+            dst_ref=out_ref.at[slot, pl.ds(part * size, size)],
+            send_sem=send_sem.at[sem, part],
+            recv_sem=recv_sem.at[sem, part],
             device_id={"ctx": target},
             device_id_type=pl.DeviceIdType.MESH,
         )
         copy.start()
         return copy
 
-    far = send(in_ref, me, 1, across)
-    near = send(in_ref, me, 2, partner)
+    mine = [in_ref.at[pl.ds(part * size, size)] for part in range(chunks)]
+    far = [send(mine[part], me, 0, part, across) for part in range(chunks)]
+    near = [send(mine[part], me, 1, part, partner) for part in range(chunks)]
     out_ref[pl.ds(me, 1)] = in_ref[...][None]
-    far.wait_recv()
-    handed = send(out_ref.at[across], across, 3, partner)
-    far.wait_send()
-    near.wait()
-    handed.wait()
-
-
-def ctx_call(kernel, block, out_shape, ident):
+    handed = []
+    for part in range(chunks):
+        far[part].wait_recv()
+        landed = out_ref.at[across, pl.ds(part * size, size)]
+        handed.append(send(landed, across, 2, part, partner))
+    for part in range(chunks):
+        far[part].wait_send()
+        near[part].wait()
+        handed[part].wait()
+
+
+def fold_kernel(count, in_ref, out_ref, near_in, held, far_in, send_sem, recv_sem):
+    me = greet_all(count)
+    even = lax.rem(me, 2)
+    partner = me + 1 - 2 * even
+    across = lax.rem(me + 2, 4)
+    corner = lax.rem(partner + 2, 4)
+    chunks = send_sem.shape[1]
+    size = in_ref.shape[1] // chunks
+
+    def send(source, dest, sem, part, target):
+        copy = pltpu.make_async_remote_copy(
+            src_ref=source,
+            dst_ref=dest,
+            send_sem=send_sem.at[sem, part],
+            recv_sem=recv_sem.at[sem, part],
+            device_id={"ctx": target},
+            device_id_type=pl.DeviceIdType.MESH,
+        )
+        copy.start()
+        return copy
+
+    spans = [pl.ds(part * size, size) for part in range(chunks)]
+    first = [
+        send(in_ref.at[corner, s], near_in.at[0, s], 0, part, partner)
+        for part, s in enumerate(spans)
+    ]
+    own = [
+        send(in_ref.at[partner, s], near_in.at[1, s], 1, part, partner)
+        for part, s in enumerate(spans)
+    ]
+    far = []
+    for part, s in enumerate(spans):
+        first[part].wait_recv()
+        held[s] = (
+            in_ref[across, s].astype(jnp.float32) + near_in[0, s].astype(jnp.float32)
+        ).astype(held.dtype)
+        far.append(send(held.at[s], far_in.at[s], 2, part, across))
+    for part, s in enumerate(spans):
+        own[part].wait_recv()
+        out_ref[s] = in_ref[me, s].astype(jnp.float32) + near_in[1, s].astype(jnp.float32)
+    for part, s in enumerate(spans):
+        far[part].wait_recv()
+        out_ref[s] = out_ref[s] + far_in[s].astype(jnp.float32)
+    for part in range(chunks):
+        first[part].wait_send()
+        own[part].wait_send()
+        far[part].wait_send()
+
+
+def chunk_count(rows):
+    return 4 if rows % 64 == 0 else 1
+
+
+def ctx_call(kernel, block, out_shape, ident, out_dtype=None, chunks=1, scratch=()):
     count = lax.axis_size("ctx")
     return pl.pallas_call(
         functools.partial(kernel, count),
-        out_shape=jax.ShapeDtypeStruct(out_shape, block.dtype),
+        out_shape=jax.ShapeDtypeStruct(out_shape, out_dtype or block.dtype),
         in_specs=[pl.BlockSpec(memory_space=pltpu.VMEM)],
         out_specs=pl.BlockSpec(memory_space=pltpu.VMEM),
         scratch_shapes=[
-            pltpu.SemaphoreType.DMA((count,)),
-            pltpu.SemaphoreType.DMA((count,)),
+            *scratch,
+            pltpu.SemaphoreType.DMA((count, chunks) if chunks else (count,)),
+            pltpu.SemaphoreType.DMA((count, chunks) if chunks else (count,)),
         ],
         compiler_params=pltpu.CompilerParams(collective_id=ident, has_side_effects=True),
         name=f"ctx_exchange_{ident}",
@@ -166,13 +228,41 @@
 
 
 def ctx_swap(block, ident):
-    return ctx_call(swap_kernel, block, block.shape, ident)
+    return ctx_call(swap_kernel, block, block.shape, ident, chunks=0)
 
 
 def ctx_share(block, ident):
     count = lax.axis_size("ctx")
-    kernel = relay_kernel if count == 4 else share_kernel
-    return ctx_call(kernel, block, (count,) + block.shape, ident)
+    if count != 4:
+        return ctx_call(share_kernel, block, (count,) + block.shape, ident, chunks=0)
+    flat = block.reshape(-1, block.shape[-1])
+    whole = ctx_call(
+        relay_kernel, flat, (count,) + flat.shape, ident, chunks=chunk_count(flat.shape[0])
+    )
+    return whole.reshape((count,) + block.shape)
+
+
+def ctx_sum(block, ident):
+    count = lax.axis_size("ctx")
+    if count != 4:
+        return jnp.sum(ctx_swap(block, ident).astype(jnp.float32), axis=0)
+    shape = block.shape[1:]
+    flat = block.reshape(count, -1, shape[-1])
+    rows, wide = flat.shape[1:]
+    total = ctx_call(
+        fold_kernel,
+        flat,
+        (rows, wide),
+        ident,
+        out_dtype=jnp.float32,
+        chunks=chunk_count(rows),
+        scratch=(
+            pltpu.VMEM((2, rows, wide), block.dtype),
+            pltpu.VMEM((rows, wide), block.dtype),
+            pltpu.VMEM((rows, wide), block.dtype),
+        ),
+    )
+    return total.reshape(shape)
 
 
 def owners_kernel(count, *refs):
@@ -375,7 +465,7 @@
 
     mixed_c = ctx_swap(to_columns(mixed.reshape(rows, width)), 2).reshape(tokens, slab)
     out_part = jnp.dot(mixed_c, out_c, preferred_element_type=jnp.float32).astype(low).reshape(ctx, rows, width)
-    out_sum = jnp.sum(ctx_swap(out_part, 3).astype(jnp.float32), axis=0)
+    out_sum = ctx_sum(out_part, 3)
     residual = inputs + (out_sum + full_bias_out)
     scaled_two, inverse_two, normed_two = norm_forward(residual, gain_two, shift_two)
     up_float = upstream.astype(jnp.float32)
@@ -391,9 +481,7 @@
     ) * gelu_slope(hidden_pre)
     grad_hidden_low = grad_hidden.astype(low)
     normed_part = outer_cols(grad_hidden_low, up_c).astype(low).reshape(ctx, rows, width)
-    sums = jnp.sum(
-        ctx_swap(jnp.stack([down_part, normed_part], axis=1), 5).astype(jnp.float32), axis=0
-    )
+    sums = ctx_sum(jnp.stack([down_part, normed_part], axis=1), 5)
     down_grad = inner_rows(upstream_all, hidden).astype(low)
     up_grad = columns_split(inner_rows(normed_two_all, grad_hidden_low), w_up)
     down_grad, up_grad, sums = lax.optimization_barrier((down_grad, up_grad, sums))
@@ -431,12 +519,12 @@
         return part.transpose(1, 0, 2, 3).reshape(ctx, rows, width)
 
     pairs = jnp.stack([to_blocks(key_part), to_blocks(value_part)], axis=1)
-    kv_sums = jnp.sum(ctx_swap(pairs, 8).astype(jnp.float32), axis=0)
+    kv_sums = ctx_sum(pairs, 8)
     grad_keys, grad_values = kv_sums[0], kv_sums[1]
     grad_projected = jnp.concatenate([grad_queries, grad_keys, grad_values], axis=1).astype(low)
     grad_projected_c = ctx_swap(to_columns(grad_projected), 9).reshape(tokens, span)
     one_part = outer_cols(grad_projected_c, qkv_c).astype(low).reshape(ctx, rows, width)
-    grad_normed_one = jnp.sum(ctx_swap(one_part, 10).astype(jnp.float32), axis=0)
+    grad_normed_one = ctx_sum(one_part, 10)
     grad_input = grad_residual + norm_backward(grad_normed_one, scaled_one, inverse_one, gain_one)
     grad_input = grad_input.reshape(seq_count, block_len, width)
 

time: 599 us -> 528 us (0.88)
  Pallas kernels: 282 us -> 250 us
  local copies, waits for them, and re-layouts: 118 us -> 92.2 us
  other arithmetic: 44.4 us -> 36.8 us
    pallas_call x12, Pallas kernels: 210 us -> 178 us  [ctx_call(): pl.pallas_call(functools.partial(kernel, count), out_shape=jax.ShapeDtype...]
    reduce_sum x4 -> x2, other arithmetic: 8.78 us -> 0.1 us  [the longest x1 0.06 us: on_device(): jnp.sum(up_float, axis=0)]
  transfers between devices with their start and end apart: 9 -> 9, of which waited for: 5 -> 5; matrix products, arithmetic and copies ran while one was open for 30% -> 29% of each run, Pallas kernels for 43% -> 44%
where the time goes in v3:
time: 528 us; the launch traced here: 521 us
  Pallas kernels  250 us (47%)
  local copies, waits for them, and re-layouts  92.2 us (17%)
  waiting for transfers between devices  59.3 us (11%)
  matrix products  51.8 us (10%)
  other arithmetic  36.8 us (7%)
  starting transfers between devices  15.6 us (3%)
  between operations  15.1 us (3%)
    pallas_call x12, Pallas kernels, ctx_call(): pl.pallas_call(functools.partial(kernel, count), out_shape=jax.ShapeDtype...  178 us
    pallas_call x1, Pallas kernels, to_owners(): pl.pallas_call(functools.partial(owners_kernel, count), out_shape=[jax.Sh...  72.5 us
    ppermute x1, waiting for transfers between devices, columns_whole(): moved = lax.ppermute(piece, ('dp', 'ctx'), there)  26.6 us
    ppermute x2, waiting for transfers between devices, columns_back(): lax.ppermute(mine.astype(low), ('dp', 'ctx'), back).astype(jnp.float32)  24.1 us
    dot_general x4, matrix products, outer_cols(): lax.dot_general(left, right, (((1,), (1,)), ((), ())), preferred_element_...  11.7 us
    dot_general x4, matrix products, inner_rows(): lax.dot_general(left, right, (((0,), (0,)), ((), ())), preferred_element_...  11.7 us
  transfers between devices with their start and end apart: 9, of which 5 were waited for; matrix products, arithmetic and copies ran while one was open for 29% of the time, Pallas kernels for 44%

profile of v3, /device:TPU:19, one launch (start us, length us, event | category | flops | bytes accessed | tf_op | source)
XLA Modules:
  0.0 521.1 jit_solution(11908624711434098518)
XLA Ops:
  11.0 5.5 %concatenate.28 = bf16[1632]{0:T(1024)(128)(2,1)S(1)} concatenate(bf16[136]{0:T(256)(128)(2,1)} %param.15, bf16[136]{0:T(256)(128)(2,1)} %param.16, bf16[272]{0:T(512)(128)(2,1)} %param.18, bf16[136]{0:T(256)(128)(2,1)} %param.20, bf16[136]{0:T(256)(128)(2,1)} %param.21, bf16[136]{0:T(256)(128)(2,1)} %param.22, bf16[544]{0:T(1024)(128)(2,1)} %param.24, bf16[136]{0:T(256)(128)(2,1)} %param.26), dimensions={0} | concatenate | bytes 6528 | tf_op jit(solution)/shard_map/concatenate | solution.py:391
  17.5 7.3 %collective-permute-done = bf16[272,408]{1,0:T(8,128)(2,1)S(1)} collective-permute-done((bf16[272,408]{1,0:T(8,128)(2,1)}, bf16[272,408]{1,0:T(8,128)(2,1)S(1)}, u32[]{:S(2)}, u32[]{:S(2)}) %collective-permute-start) | collective-permute-done | bytes 221984 | tf_op jit(solution)/shard_map/ppermute | solution.py:394
  29.4 26.6 %collective-permute-done.1 = bf16[272,544]{1,0:T(8,128)(2,1)S(1)} collective-permute-done((bf16[272,544]{1,0:T(8,128)(2,1)}, bf16[272,544]{1,0:T(8,128)(2,1)S(1)}, u32[]{:S(2)}, u32[]{:S(2)}) %collective-permute-start.1) | collective-permute-done | bytes 295968 | tf_op jit(solution)/shard_map/ppermute | solution.py:366
  58.9 19.3 %ctx_exchange_0.1 = bf16[4,256,1088]{2,1,0:T(8,128)(2,1)} custom-call(bf16[256,1088]{1,0:T(8,128)(2,1)} %bitcast.264), custom_call_target="tpu_custom_call" | custom-call | tf_op jit(solution)/shard_map/ctx_exchange_0/pallas_call | solution.py:215
  101.4 6.0 %reshape.409 = bf16[1088,816]{1,0:T(8,128)(2,1)} reshape(bf16[4,272,2,408]{3,2,1,0:T(2,128)(2,1)} %bitcast.242) | data formatting | bytes 3551232 | tf_op jit(solution)/shard_map/reshape | solution.py:363
  111.5 28.5 %ctx_exchange_1.1 = bf16[4,512,816]{2,1,0:T(8,128)(2,1)} custom-call(bf16[512,816]{1,0:T(8,128)(2,1)} %add_convert_fusion.2.in_ref), custom_call_target="tpu_custom_call" | custom-call | tf_op jit(solution)/shard_map/ctx_exchange_1/pallas_call | solution.py:215
  140.0 6.8 %copy.113 = bf16[4,4,1,128,816]{3,1,4,0,2:T(4,128)(2,1)} copy(bf16[4,4,1,128,816]{4,3,1,0,2:T(8,128)(2,1)} %bitcast.229) | data formatting | bytes 6684672 | tf_op jit(solution)/shard_map/reshape | solution.py:439
  146.8 5.4 %reshape.411 = bf16[1,512,3264]{1,2,0:T(8,128)(2,1)S(1)} reshape(bf16[1,4,128,4,816]{2,1,4,3,0:T(4,128)(2,1)} %bitcast.230) | data formatting | bytes 6684672 | tf_op jit(solution)/shard_map/reshape | solution.py:441
  158.0 8.9 %ctx_exchange_2.1 = bf16[4,128,272]{2,1,0:T(8,128)(2,1)} custom-call(bf16[4,128,272]{2,1,0:T(8,128)(2,1)} %bitcast.268), custom_call_target="tpu_custom_call" | custom-call | tf_op jit(solution)/shard_map/ctx_exchange_2/pallas_call | solution.py:215
  170.5 12.4 %ctx_exchange_3.1 = f32[128,1088]{1,0:T(8,128)} custom-call(bf16[4,128,1088]{2,1,0:T(8,128)(2,1)} %bitcast.247), custom_call_target="tpu_custom_call" | custom-call | tf_op jit(solution)/shard_map/ctx_exchange_3/pallas_call | solution.py:215
  185.9 12.9 %ctx_exchange_4.1 = bf16[4,128,1088]{2,1,0:T(8,128)(2,1)} custom-call(bf16[128,1088]{1,0:T(8,128)(2,1)} %add_convert_fusion.3.in_ref), custom_call_target="tpu_custom_call" | custom-call | tf_op jit(solution)/shard_map/ctx_exchange_4/pallas_call | solution.py:215
  212.8 5.3 %fusion.49 = (f32[1088]{0:T(1024)}, bf16[512,1088]{0,1:T(8,128)(2,1)S(1)}, f32[512,1088]{0,1:T(8,128)S(1)}) fusion(f32[512,1088]{0,1:T(8,128)S(1)} %convolution_add_fusion, bf16[512,1088]{1,0:T(8,128)(2,1)} %bitcast.270, bf16[1088,1088]{1,0:T(8,128)(2,1)} %all-gather.7.cloned.1.call-done), kind=kOutput, calls=%fused_computation.129 | convolution fusion | flops 1219394560 | bytes 9056512 | tf_op jit(solution)/shard_map/dot_general | solution.py:479
  233.9 19.5 %ctx_exchange_5.1 = f32[256,1088]{1,0:T(8,128)} custom-call(bf16[4,256,1088]{2,1,0:T(8,128)(2,1)} %bitcast.238), custom_call_target="tpu_custom_call" | custom-call | tf_op jit(solution)/shard_map/ctx_exchange_5/pallas_call | solution.py:215
  267.0 13.0 %ctx_exchange_6.1 = bf16[4,128,1088]{2,1,0:T(8,128)(2,1)} custom-call(bf16[128,1088]{1,0:T(8,128)(2,1)} %convert_element_type.253.in_ref), custom_call_target="tpu_custom_call" | custom-call | tf_op jit(solution)/shard_map/ctx_exchange_6/pallas_call | solution.py:215
  283.0 8.9 %ctx_exchange_7.1 = bf16[4,128,272]{2,1,0:T(8,128)(2,1)} custom-call(bf16[4,128,272]{2,1,0:T(8,128)(2,1)} %bitcast.266), custom_call_target="tpu_custom_call" | custom-call | tf_op jit(solution)/shard_map/ctx_exchange_7/pallas_call | solution.py:215
  293.8 4.5 multiply_convert_fusion
  324.5 19.5 %ctx_exchange_8.1 = f32[256,1088]{1,0:T(8,128)} custom-call(bf16[4,256,1088]{2,1,0:T(8,128)(2,1)} %bitcast.239), custom_call_target="tpu_custom_call" | custom-call | tf_op jit(solution)/shard_map/ctx_exchange_8/pallas_call | solution.py:215
  349.1 15.3 %ctx_exchange_9.1 = bf16[4,128,816]{2,1,0:T(8,128)(2,1)} custom-call(bf16[4,128,816]{2,1,0:T(8,128)(2,1)} %bitcast.253), custom_call_target="tpu_custom_call" | custom-call | tf_op jit(solution)/shard_map/ctx_exchange_9/pallas_call | solution.py:215
  369.3 12.5 %ctx_exchange_10.1 = f32[128,1088]{1,0:T(8,128)} custom-call(bf16[4,128,1088]{2,1,0:T(8,128)(2,1)} %bitcast.248), custom_call_target="tpu_custom_call" | custom-call | tf_op jit(solution)/shard_map/ctx_exchange_10/pallas_call | solution.py:215
  384.1 7.1 %ctx_exchange_11.1 = f32[4,8,1632]{2,1,0:T(8,128)} custom-call(f32[8,1632]{1,0:T(8,128)} %concatenate.35.in_ref), custom_call_target="tpu_custom_call" | custom-call | tf_op jit(solution)/shard_map/ctx_exchange_11/pallas_call | solution.py:215
  398.0 72.5 %dp_owners_12.1 = (bf16[8,272,408]{2,1,0:T(8,128)(2,1)}, bf16[8,136,272]{2,1,0:T(8,128)(2,1)}, f32[8,1,1632]{2,1,0:T(1,128)}) custom-call(bf16[8,272,408]{2,1,0:T(8,128)(2,1)} %bitcast.265, bf16[8,136,272]{2,1,0:T(8,128)(2,1)} %bitcast.255, f32[8,1,1632]{2,1,0:T(1,128)} %broadcast_in_dim.18.refs_2_), custom_call_target="tpu_custom_call" | custom-call | tf_op jit(solution)/shard_map/dp_owners_12/pallas_call | solution.py:312
  477.0 5.8 %collective-permute-start.2 = (bf16[272,408]{1,0:T(8,128)(2,1)S(1)}, bf16[272,408]{1,0:T(8,128)(2,1)S(1)}, u32[]{:S(2)}, u32[]{:S(2)}) collective-permute-start(bf16[272,408]{1,0:T(8,128)(2,1)S(1)} %reduce_sum.241), channel_id=1, source_target_pairs={{0,0},{8,1},{16,2},{24,3},{4,4},{12,5},{20,6},{28,7},{1,8},{9,9},{... | collective-permute-start | bytes 665864 | tf_op jit(solution)/shard_map/ppermute | solution.py:374
  484.3 11.2 %collective-permute-done.2 = bf16[272,408]{1,0:T(8,128)(2,1)S(1)} collective-permute-done((bf16[272,408]{1,0:T(8,128)(2,1)S(1)}, bf16[272,408]{1,0:T(8,128)(2,1)S(1)}, u32[]{:S(2)}, u32[]{:S(2)}) %collective-permute-start.2) | collective-permute-done | bytes 221984 | tf_op jit(solution)/shard_map/ppermute | solution.py:374
  500.6 12.9 %collective-permute-done.3 = bf16[272,544]{1,0:T(8,128)(2,1)S(1)} collective-permute-done((bf16[272,544]{1,0:T(8,128)(2,1)}, bf16[272,544]{1,0:T(8,128)(2,1)S(1)}, u32[]{:S(2)}, u32[]{:S(2)}) %collective-permute-start.3) | collective-permute-done | bytes 295968 | tf_op jit(solution)/shard_map/ppermute | solution.py:374
  (280 shorter events, 158.3 us)
Async XLA Ops:
  7.2 50.3 %copy-start.30 = (bf16[1,128,1088]{1,2,0:T(8,128)(2,1)S(1)}, bf16[1,128,1088]{1,2,0:T(8,128)(2,1)}, u32[]{:S(2)}) copy-start(bf16[1,128,1088]{1,2,0:T(8,128)(2,1)} %param.14) | copy-start | bytes 835588
  7.2 50.5 %copy-start.31 = (bf16[1,128,1088]{1,2,0:T(8,128)(2,1)S(1)}, bf16[1,128,1088]{1,2,0:T(8,128)(2,1)}, u32[]{:S(2)}) copy-start(bf16[1,128,1088]{1,2,0:T(8,128)(2,1)} %param.27) | copy-start | bytes 835588
  7.2 79.3 %all-gather.11.cloned.1.call-start = ((), (), s32[]{:S(2)}) async-start(), calls=%async_computation.5 | async-start | bytes 3225600 | tf_op jit(solution)/shard_map/all_gather | solution.py:396
  7.2 17.6 %collective-permute-start = (bf16[272,408]{1,0:T(8,128)(2,1)}, bf16[272,408]{1,0:T(8,128)(2,1)S(1)}, u32[]{:S(2)}, u32[]{:S(2)}) collective-permute-start(bf16[272,408]{1,0:T(8,128)(2,1)} %param.17), channel_id=1, source_target_pairs={{0,0},{1,8},{2,16},{3,24},{4,4},{5,12},{6,20},{7,28},{8,1},{9,9},{... | collective-permute-start | bytes 665864 | tf_op jit(solution)/shard_map/ppermute | solution.py:394
  25.7 176.2 %all-gather.9.cloned.1.call-start = ((), (), s32[]{:S(2)}) async-start(), calls=%async_computation.4 | async-start | bytes 3133440 | tf_op jit(solution)/shard_map/all_gather | solution.py:367
  25.8 30.2 %collective-permute-start.1 = (bf16[272,544]{1,0:T(8,128)(2,1)}, bf16[272,544]{1,0:T(8,128)(2,1)S(1)}, u32[]{:S(2)}, u32[]{:S(2)}) collective-permute-start(bf16[272,544]{1,0:T(8,128)(2,1)} %param.23), channel_id=1, source_target_pairs={{0,0},{1,8},{2,16},{3,24},{4,4},{5,12},{6,20},{7,28},{8,1},{9,9},{... | collective-permute-start | bytes 887816 | tf_op jit(solution)/shard_map/ppermute | solution.py:366
  56.7 156.0 %all-gather.7.cloned.1.call-start = ((), (), s32[]{:S(2)}) async-start(), calls=%async_computation.2 | async-start | bytes 2820096 | tf_op jit(solution)/shard_map/all_gather | solution.py:377
  57.5 439.0 %reduce-scatter.5.cloned.1.call-start = ((), (), s32[]{:S(2)}) async-start(), calls=%async_computation.3 | async-start | bytes 3133440 | tf_op jit(solution)/shard_map/reduce_scatter | solution.py:489
  57.7 25.9 %copy-start.10 = (bf16[1,128,1088]{2,1,0:T(8,128)(2,1)}, bf16[1,128,1088]{2,1,0:T(8,128)(2,1)S(1)}, u32[]{:S(2)}) copy-start(bf16[1,128,1088]{2,1,0:T(8,128)(2,1)S(1)} %copy.107) | copy-start | bytes 835588
  83.7 71.2 %copy-start.35 = (pred[128,512]{1,0:T(8,128)(4,1)}, pred[128,512]{1,0:T(8,128)(4,1)S(1)}, u32[]{:S(2)}) copy-start(pred[128,512]{1,0:T(8,128)(4,1)S(1)} %iota_compare_fusion) | copy-start | bytes 196612
  233.8 19.6 %copy-start.28 = (bf16[1088,512]{1,0:T(8,128)(2,1)S(1)}, bf16[1088,512]{1,0:T(8,128)(2,1)}, u32[]{:S(2)}) copy-start(bf16[1088,512]{1,0:T(8,128)(2,1)} %copy.118) | copy-start | bytes 3342340
  233.8 19.6 %copy-start.29 = (bf16[1088,512]{1,0:T(8,128)(2,1)S(1)}, bf16[1088,512]{1,0:T(8,128)(2,1)}, u32[]{:S(2)}) copy-start(bf16[1088,512]{1,0:T(8,128)(2,1)} %fusion.8) | copy-start | bytes 3342340
  256.7 242.1 %reduce-scatter.7.cloned.1.call-start = ((), (), s32[]{:S(2)}) async-start(), calls=%async_computation.6 | async-start | bytes 2820096
  264.7 15.4 %copy-start.9 = (bf16[272,8,136]{0,2,1:T(8,128)(2,1)S(1)}, bf16[272,8,136]{0,2,1:T(8,128)(2,1)}, u32[]{:S(2)}) copy-start(bf16[272,8,136]{0,2,1:T(8,128)(2,1)} %copy.115) | copy-start | bytes 1775620
  367.6 15.8 %copy-start.39 = (f32[8,544]{1,0:T(8,128)S(1)}, f32[8,544]{1,0:T(8,128)}, u32[]{:S(2)}) copy-start(f32[8,544]{1,0:T(8,128)} %reshape.439) | copy-start | bytes 52228
  367.6 15.8 %copy-start.52 = (f32[8,136]{1,0:T(8,128)S(1)}, f32[8,136]{1,0:T(8,128)}, u32[]{:S(2)}) copy-start(f32[8,136]{1,0:T(8,128)} %reshape.440) | copy-start | bytes 13060
  367.6 15.8 %copy-start.53 = (f32[8,136]{1,0:T(8,128)S(1)}, f32[8,136]{1,0:T(8,128)}, u32[]{:S(2)}) copy-start(f32[8,136]{1,0:T(8,128)} %reshape.437) | copy-start | bytes 13060
  367.6 15.8 %copy-start.54 = (f32[8,136]{1,0:T(8,128)S(1)}, f32[8,136]{1,0:T(8,128)}, u32[]{:S(2)}) copy-start(f32[8,136]{1,0:T(8,128)} %reshape.436) | copy-start | bytes 13060
  369.3 23.6 %copy-start.14 = (bf16[4,128,816]{2,1,0:T(8,128)(2,1)S(1)}, bf16[4,128,816]{2,1,0:T(8,128)(2,1)}, u32[]{:S(2)}) copy-start(bf16[4,128,816]{2,1,0:T(8,128)(2,1)} %ctx_exchange_9.1) | copy-start | bytes 2506756
  369.3 24.8 %copy-start.27 = (bf16[512,1088]{0,1:T(8,128)(2,1)S(1)}, bf16[512,1088]{0,1:T(8,128)(2,1)}, u32[]{:S(2)}) copy-start(bf16[512,1088]{0,1:T(8,128)(2,1)} %add_convert_fusion.1) | copy-start | bytes 3342340
  398.0 74.7 %copy-start.24 = (bf16[1,128,1088]{2,1,0:T(8,128)(2,1)S(1)}, bf16[1,128,1088]{2,1,0:T(8,128)(2,1)}, u32[]{:S(2)}) copy-start(bf16[1,128,1088]{2,1,0:T(8,128)(2,1)} %get-tuple-element.100) | copy-start | bytes 835588
  398.0 75.6 %copy-start.13 = (f32[128,1088]{1,0:T(8,128)S(1)}, f32[128,1088]{1,0:T(8,128)}, u32[]{:S(2)}) copy-start(f32[128,1088]{1,0:T(8,128)} %ctx_exchange_10.1) | copy-start | bytes 1671172
  477.0 18.6 %collective-permute-start.2 = (bf16[272,408]{1,0:T(8,128)(2,1)S(1)}, bf16[272,408]{1,0:T(8,128)(2,1)S(1)}, u32[]{:S(2)}, u32[]{:S(2)}) collective-permute-start(bf16[272,408]{1,0:T(8,128)(2,1)S(1)} %reduce_sum.241), channel_id=1, source_target_pairs={{0,0},{8,1},{16,2},{24,3},{4,4},{12,5},{20,6},{28,7},{1,8},{9,9},{... | collective-permute-start | bytes 665864 | tf_op jit(solution)/shard_map/ppermute | solution.py:374
  496.4 17.0 %collective-permute-start.3 = (bf16[272,544]{1,0:T(8,128)(2,1)}, bf16[272,544]{1,0:T(8,128)(2,1)S(1)}, u32[]{:S(2)}, u32[]{:S(2)}) collective-permute-start(bf16[272,544]{1,0:T(8,128)(2,1)} %bitcast.281), channel_id=1, source_target_pairs={{0,0},{8,1},{16,2},{24,3},{4,4},{12,5},{20,6},{28,7},{1,8},{9,9},{... | collective-permute-start | bytes 887816 | tf_op jit(solution)/shard_map/ppermute | solution.py:374
  (50 other events, 285.4 us)
Sparse Core Ops, SparseCore 0:
  25.9 60.5 all-gather.10
  89.2 54.7 all-gather.8
  146.2 51.7 all-gather.6
  256.8 71.4 reduce-scatter.4
  331.7 69.6 reduce-scatter.6
